TPU v7x, 256 devices: a whole 4x4x8 slice. The times are simulated.
256 devices in a mesh: row: 16 (over x, z_lo, core), col: 16 (over y, z_hi).
Axes of the slice: x: 4, y: 4, z: 8 (z_hi: 4, z_lo: 2; z = z_hi * 2 + z_lo), core: 2. Of those that a mesh axis runs over, the one named last changes fastest.
Arguments:
- swath: int32 [2560, 8192], P('row', 'col'), may hold values from 0 to 1
- coherence: int32 [2560, 8192], P('row', 'col'), may hold values from 0 to 7
- phase_counts: int32 [2560, 8192], P('row', 'col'), may hold values from 0 to 255
Outputs:
- unwrapped: float32 [2560, 8192], P('row', 'col')
All inputs are finite; a program needn't handle non-finite values.
Results may differ from a plain program's by a relative error of at most 0.0012.
Values sent between devices are 32-bit elements; how exact they have to be, the bound alone decides.
A program may use at most 128 MiB of HBM per device.

v0:
```python
import functools

import jax
import jax.numpy as jnp
from jax import lax
from jax.sharding import Mesh
from jax.sharding import PartitionSpec as P

GRIDS = 4
LEVELS = 256
NCLASS = 8
ROW_COL = ("row_0", "row_1", "row_2", "col_0", "col_1")
ROW = ("row_0", "row_1", "row_2")
COL = ("col_0", "col_1")


damping = 0.8
diag_floor = 0.5
error_floor = 0.5
epsilon = 1e-06
screen_width = 4.0
highest = lax.Precision.HIGHEST


def with_halo(x, sides, width):
    edges = {}
    for axis, dim in sides:
        devices, length = (lax.axis_size(axis), x.shape[dim])
        up = [(i, (i + 1) % devices) for i in range(devices - 1)]
        last = lax.slice_in_dim(x, length - width, length, axis=dim)
        leading = lax.slice_in_dim(x, 0, width, axis=dim)
        edges[dim] = (
            lax.ppermute(last, axis, up),
            lax.ppermute(leading, axis, [(b, a) for a, b in up]),
        )
    done = []
    for _, dim in sides:
        low, high = edges[dim]
        around = [(width, width) if d in done else (0, 0) for d in range(x.ndim)]
        x = jnp.concatenate([jnp.pad(low, around), x, jnp.pad(high, around)], axis=dim)
        done.append(dim)
    return x


def over_axes(x, axes):
    return functools.reduce(lax.psum, axes, x)


def in_order(tiles, dim):
    lengths = list(tiles.shape[1:])
    lengths[dim] *= tiles.shape[0]
    return jnp.moveaxis(tiles, 0, dim).reshape(lengths)


def from_everyone(x, axis):
    copies = jnp.broadcast_to(x, (lax.axis_size(axis), *x.shape))
    return lax.all_to_all(copies, axis, split_axis=0, concat_axis=0, tiled=True)


def gathered_copies(x, axis, dim):
    return in_order(from_everyone(x, axis), dim)


def from_behind(value, axis, steps):
    count = lax.axis_size(axis)
    leading, last = (max(0, -steps), min(count, count - steps))
    return lax.ppermute(value, axis, [(source, source + steps) for source in range(leading, last)])


def cosine_table(count):
    freq = jnp.arange(count, dtype=jnp.float32)[:, None]
    place = jnp.arange(count, dtype=jnp.float32)[None, :]
    table = jnp.cos(jnp.pi * (place + 0.5) * freq / count) * jnp.sqrt(2.0 / count)
    return jnp.where(freq == 0, table * jnp.sqrt(0.5), table)


def eigen_values(freq, count):
    return 2.0 - 2.0 * jnp.cos(jnp.pi * freq / count)


def product(first, second):
    return jnp.dot(first, second, precision=highest)


def contract_first(first, second):
    return lax.dot_general(first, second, (((0,), (0,)), ((), ())), precision=highest)


def contract_last(first, second):
    return lax.dot_general(first, second, (((1,), (1,)), ((), ())), precision=highest)


def neighbours(estimate):
    return with_halo(estimate, ((ROW, 0), (COL, 1)), 1)


def weight_diagonal(w_down_pad, w_right_pad):
    return w_down_pad[1:] + w_down_pad[:-1] + w_right_pad[:, 1:] + w_right_pad[:, :-1]


def operate(padded, estimate, w_down_pad, w_right_pad, diagonal):
    beside = (
        w_down_pad[1:] * padded[2:, 1:-1]
        + w_down_pad[:-1] * padded[:-2, 1:-1]
        + w_right_pad[:, 1:] * padded[1:-1, 2:]
        + w_right_pad[:, :-1] * padded[1:-1, :-2]
    )
    return diagonal * estimate - beside


def prolongate(field):
    return jnp.repeat(jnp.repeat(field, 2, axis=0), 2, axis=1)


def coarse_weights(w_down_pad, w_right_pad):
    w_down = w_down_pad[1:]
    w_up = w_down_pad[:-1]
    lower = w_down[1::2, 0::2] + w_down[1::2, 1::2]
    upper = w_up[0:1, 0::2] + w_up[0:1, 1::2]
    w_right = w_right_pad[:, 1:]
    w_left = w_right_pad[:, :-1]
    rightward = w_right[0::2, 1::2] + w_right[1::2, 1::2]
    leftward = w_left[0::2, 0:1] + w_left[1::2, 0:1]
    return (jnp.concatenate([upper, lower], 0), jnp.concatenate([leftward, rightward], 1))


def coarse_solve(source, w_down_pad, w_right_pad):
    rows_here, cols_here = source.shape
    row_count = lax.axis_size(ROW)
    col_count = lax.axis_size(COL)
    grid_rows = rows_here * row_count
    grid_cols = cols_here * col_count
    local = jnp.sum(w_down_pad[1:]) + jnp.sum(w_right_pad[:, 1:])
    total = over_axes(local, ROW_COL)
    count = (grid_rows - 1) * grid_cols + grid_rows * (grid_cols - 1)
    mean = total / count + epsilon
    screen = (screen_width / grid_cols) ** 2
    table_x = cosine_table(grid_rows)
    table_y = cosine_table(grid_cols)
    row_index = lax.axis_index(ROW)
    col_index = lax.axis_index(COL)
    strip = gathered_copies(source, COL, 1)
    spectrum = contract_last(strip, table_y)
    spectrum = lax.all_to_all(spectrum, ROW, split_axis=1, concat_axis=0, tiled=True)
    spectrum = product(table_x, spectrum)
    block = grid_cols // row_count
    freq_y = (row_index * block + jnp.arange(block, dtype=jnp.int32)).astype(jnp.float32)
    lam_x = eigen_values(jnp.arange(grid_rows, dtype=jnp.float32), grid_rows)
    lam_y = eigen_values(freq_y, grid_cols)
    spectrum = spectrum / (mean * (lam_x[:, None] + lam_y[None, :] + screen))
    values = contract_first(table_x, spectrum)
    values = lax.all_to_all(values, ROW, split_axis=0, concat_axis=1, tiled=True)
    strip = product(values, table_y)
    return lax.dynamic_slice_in_dim(strip, col_index * cols_here, cols_here, 1)


def cycle(estimate, source, w_down_pad, w_right_pad, depth, padded):
    if depth == GRIDS:
        return coarse_solve(source, w_down_pad, w_right_pad)
    diagonal = weight_diagonal(w_down_pad, w_right_pad)
    divisor = jnp.maximum(diagonal, diag_floor)
    if estimate is None:
        estimate = damping * source / divisor
    else:
        estimate = (
            estimate
            + damping
            * (source - operate(padded, estimate, w_down_pad, w_right_pad, diagonal))
            / divisor
        )
    padded = neighbours(estimate)
    residual = source - operate(padded, estimate, w_down_pad, w_right_pad, diagonal)
    rows, cols = residual.shape
    coarse_source = residual.reshape(rows // 2, 2, cols // 2, 2).sum(axis=(1, 3))
    down_next, right_next = coarse_weights(w_down_pad, w_right_pad)
    correction = cycle(None, coarse_source, down_next, right_next, depth + 1, None)
    estimate = estimate + prolongate(correction)
    padded = neighbours(estimate)
    return (
        estimate
        + damping
        * (source - operate(padded, estimate, w_down_pad, w_right_pad, diagonal))
        / divisor
    )


def faces(w_down, w_right, slope_down, slope_right):
    flux_down = w_down * slope_down
    flux_right = w_right * slope_right
    above = from_behind(jnp.stack([w_down[-1], flux_down[-1]]), ROW, 1)
    before = from_behind(jnp.stack([w_right[:, -1], flux_right[:, -1]]), COL, 1)
    w_down_pad = jnp.concatenate([above[0:1], w_down], 0)
    w_right_pad = jnp.concatenate([before[0][:, None], w_right], 1)
    flux_up = jnp.concatenate([above[1:2], flux_down[:-1]], 0)
    flux_left = jnp.concatenate([before[1][:, None], flux_right[:, :-1]], 1)
    source = flux_up - flux_down + flux_left - flux_right
    return (source, w_down_pad, w_right_pad)


def wrap_steps(difference):
    half = LEVELS // 2
    return (jnp.mod(difference + half, LEVELS) - half) * (2.0 * jnp.pi / LEVELS)


def body(swath, coherence, phase_counts):
    quality = swath.astype(jnp.float32) * (coherence.astype(jnp.float32) / (NCLASS - 1)) ** 2
    counts = phase_counts.astype(jnp.float32)
    below = from_behind(jnp.stack([quality[0], counts[0]]), ROW, -1)
    after = from_behind(jnp.stack([quality[:, 0], counts[:, 0]]), COL, -1)
    quality_below = jnp.concatenate([quality[1:], below[0:1]], 0)
    counts_below = jnp.concatenate([counts[1:], below[1:2]], 0)
    quality_after = jnp.concatenate([quality[:, 1:], after[0][:, None]], 1)
    counts_after = jnp.concatenate([counts[:, 1:], after[1][:, None]], 1)
    w_down = jnp.minimum(quality, quality_below)
    w_right = jnp.minimum(quality, quality_after)
    slope_down = wrap_steps(counts_below - counts)
    slope_right = wrap_steps(counts_after - counts)
    source, w_down_pad, w_right_pad = faces(w_down, w_right, slope_down, slope_right)
    first = cycle(None, source, w_down_pad, w_right_pad, 0, None)
    padded = neighbours(first)
    error_down = padded[2:, 1:-1] - first - slope_down
    error_right = padded[1:-1, 2:] - first - slope_right
    reweighted_down = w_down / jnp.maximum(jnp.abs(error_down), error_floor)
    reweighted_right = w_right / jnp.maximum(jnp.abs(error_right), error_floor)
    source, w_down_pad, w_right_pad = faces(
        reweighted_down, reweighted_right, slope_down, slope_right
    )
    return cycle(first, source, w_down_pad, w_right_pad, 0, padded)


def solution(mesh):
    finer = Mesh(mesh.devices.reshape(4, 2, 2, 4, 4), ("row_0", "row_1", "row_2", "col_0", "col_1"))
    return jax.shard_map(
        body,
        mesh=finer,
        in_specs=(P(ROW, COL), P(ROW, COL), P(ROW, COL)),
        out_specs=P(ROW, COL),
        check_vma=False,
    )
```

profile of v0, /device:TPU:33, one launch (start us, length us, event | category | flops | bytes accessed | tf_op | source)
XLA Modules:
  0.0 624.6 jit_solution(2693713752611302289)
XLA Ops:
  13.6 5.5 collective-permute-start.3
  34.9 5.3 collective-permute-start.1
  61.6 22.3 %reshape.177 = f32[80,2,256,2]{3,2,1,0:T(8,128)} reshape(f32[160,512]{1,0:T(8,128)S(1)} %fusion.91) | data formatting | bytes 655360 | tf_op jit(solution)/shard_map/reshape | solution.py:174
  83.9 8.8 %reduce_sum.108 = f32[80,256]{1,0:T(8,128)S(1)} reduce(f32[80,2,256,2]{3,2,1,0:T(8,128)} %reshape.177, f32[]{:T(128)} %constant.36.clone.1), dimensions={1,3}, to_apply=%region_0.1 | reduce | flops 61440 | bytes 409604 | tf_op jit(solution)/shard_map/reduce_sum | solution.py:174
  109.7 6.8 %reshape.178 = f32[40,2,128,2]{3,2,1,0:T(8,128)} reshape(f32[80,256]{1,0:T(8,128)S(1)} %fusion.154) | data formatting | bytes 163840 | tf_op jit(solution)/shard_map/reshape | solution.py:174
  157.2 6.9 %all-to-all-start = ((f32[16,1,320]{2,1,0:T(1,128)}), f32[16,1,320]{2,1,0:T(1,128)S(1)}, u32[]{:S(2)}, u32[]{:S(2)}) async-start(f32[16,1,320]{2,1,0:T(1,128)} %reshape.213), calls=%async_computation | async-start | bytes 49152 | tf_op jit(solution)/shard_map/all_to_all | solution.py:57
  166.7 9.0 %psum.70 = f32[]{:T(128)} all-reduce(f32[]{:T(128)S(6)} %add.617), channel_id=1, replica_groups=mesh['row_0'=4,'row_1'=2,'row_2'=2,'col_0'=4,'col_1'=4] {'row_0'}, use_global_device_ids=true, to_apply=%region_6.7 | all-reduce | flops 1 | bytes 8 | tf_op jit(solution)/shard_map/psum | solution.py:46
  180.0 5.9 psum.72
  185.9 9.5 %psum.73 = f32[]{:T(128)} all-reduce(f32[]{:T(128)} %psum.72), channel_id=1, replica_groups=mesh['row_0'=4,'row_1'=2,'row_2'=2,'col_0'=4,'col_1'=4] {'col_0'}, use_global_device_ids=true, to_apply=%region_9.10 | all-reduce | flops 1 | bytes 8 | tf_op jit(solution)/shard_map/psum | solution.py:46
  196.9 6.4 %fusion.365 = f32[16,10,32]{2,1,0:T(8,128)S(1)} fusion(f32[10,512,1]{1,0,2:T(8,128)S(1)} %reshape.203, f32[16,32]{1,0:T(8,128)} %multiply_add_fusion, f32[512]{0:T(512)} %add_multiply_fusion, pred[16,32]{1,0:T(8,128)(4,1)} %broadcast_compare_fusion), kind=kOutput, calls=%fused_computation.576 | convolution fusion | flops 32768000 | bytes 45568 | tf_op jit(solution)/shard_map/dot_general | solution.py:90
  204.0 7.3 %all-to-all-start.1 = ((f32[16,1,320]{2,1,0:T(1,128)}), f32[16,1,320]{2,1,0:T(1,128)S(1)}, u32[]{:S(2)}, u32[]{:S(2)}) async-start(f32[16,1,320]{2,1,0:T(1,128)} %reshape.215), calls=%async_computation.1 | async-start | bytes 49152 | tf_op jit(solution)/shard_map/all_to_all | solution.py:144
  211.3 10.7 %psum.74 = f32[]{:T(128)} all-reduce(f32[]{:T(128)} %psum.73), channel_id=1, replica_groups=mesh['row_0'=4,'row_1'=2,'row_2'=2,'col_0'=4,'col_1'=4] {'col_1'}, use_global_device_ids=true, to_apply=%region_10.11 | all-reduce | flops 1 | bytes 8 | tf_op jit(solution)/shard_map/psum | solution.py:46
  227.5 8.1 %all-to-all-start.2 = ((f32[16,1,320]{2,1,0:T(1,128)}), f32[16,1,320]{2,1,0:T(1,128)S(1)}, u32[]{:S(2)}, u32[]{:S(2)}) async-start(f32[16,1,320]{2,1,0:T(1,128)} %reshape.217), calls=%async_computation.2 | async-start | bytes 49152 | tf_op jit(solution)/shard_map/all_to_all | solution.py:152
  290.4 5.2 collective-permute-done.30
  309.0 5.7 collective-permute-done.34
  349.6 5.3 collective-permute-start.37
  359.9 5.4 collective-permute-start.43
  367.1 7.0 %collective-permute-done.44 = f32[160,1]{1,0:T(8,128)S(1)} collective-permute-done((f32[160,1]{1,0:T(8,128)S(1)}, f32[160,1]{1,0:T(8,128)S(1)}, u32[]{:S(2)}, u32[]{:S(2)}) %collective-permute-start.44) | collective-permute-done | bytes 672 | tf_op jit(solution)/shard_map/ppermute | solution.py:34
  374.4 22.3 %reshape.190 = f32[80,2,256,2]{3,2,1,0:T(8,128)} reshape(f32[160,512]{1,0:T(8,128)S(1)} %fusion.48) | data formatting | bytes 655360 | tf_op jit(solution)/shard_map/reshape | solution.py:174
  396.7 8.8 %reduce_sum.114 = f32[80,256]{1,0:T(8,128)S(1)} reduce(f32[80,2,256,2]{3,2,1,0:T(8,128)} %reshape.190, f32[]{:T(128)} %constant.36.clone.1), dimensions={1,3}, to_apply=%region_11.12 | reduce | flops 61440 | bytes 409604 | tf_op jit(solution)/shard_map/reduce_sum | solution.py:174
  423.2 6.8 %reshape.191 = f32[40,2,128,2]{3,2,1,0:T(8,128)} reshape(f32[80,256]{1,0:T(8,128)S(1)} %fusion.129) | data formatting | bytes 163840 | tf_op jit(solution)/shard_map/reshape | solution.py:174
  450.9 5.4 collective-permute-start.57
  475.0 8.0 %all-to-all-done.3 = f32[16,1,320]{2,1,0:T(1,128)S(1)} async-done(((f32[16,1,320]{2,1,0:T(1,128)}), f32[16,1,320]{2,1,0:T(1,128)S(1)}, u32[]{:S(2)}, u32[]{:S(2)}) %all-to-all-start.3) | async-done | bytes 20512 | tf_op jit(solution)/shard_map/all_to_all | solution.py:57
  484.0 5.7 fusion.366
  490.4 5.2 all-to-all-start.4
  497.4 8.9 %psum.75 = f32[]{:T(128)} all-reduce(f32[]{:T(128)S(6)} %add.692), channel_id=1, replica_groups=mesh['row_0'=4,'row_1'=2,'row_2'=2,'col_0'=4,'col_1'=4] {'row_0'}, use_global_device_ids=true, to_apply=%region_17.18 | all-reduce | flops 1 | bytes 8 | tf_op jit(solution)/shard_map/psum | solution.py:46
  510.6 6.3 %psum.77 = f32[]{:T(128)} all-reduce(f32[]{:T(128)} %psum.76), channel_id=1, replica_groups=mesh['row_0'=4,'row_1'=2,'row_2'=2,'col_0'=4,'col_1'=4] {'row_2'}, use_global_device_ids=true, to_apply=%region_19.20 | all-reduce | flops 1 | bytes 8 | tf_op jit(solution)/shard_map/psum | solution.py:46
  516.9 7.5 %psum.78 = f32[]{:T(128)} all-reduce(f32[]{:T(128)} %psum.77), channel_id=1, replica_groups=mesh['row_0'=4,'row_1'=2,'row_2'=2,'col_0'=4,'col_1'=4] {'col_0'}, use_global_device_ids=true, to_apply=%region_20.21 | all-reduce | flops 1 | bytes 8 | tf_op jit(solution)/shard_map/psum | solution.py:46
  524.4 8.0 %psum.79 = f32[]{:T(128)} all-reduce(f32[]{:T(128)} %psum.78), channel_id=1, replica_groups=mesh['row_0'=4,'row_1'=2,'row_2'=2,'col_0'=4,'col_1'=4] {'col_1'}, use_global_device_ids=true, to_apply=%region_21.22 | all-reduce | flops 1 | bytes 8 | tf_op jit(solution)/shard_map/psum | solution.py:46
  535.9 12.4 %all_to_all.80 = f32[16,1,320]{2,1,0:T(1,128)S(1)} all-to-all(f32[16,1,320]{2,1,0:T(1,128)S(1)} %reshape.223), channel_id=1, replica_groups=mesh['row_0'=4,'row_1'=2,'row_2'=2,'col_0'=4,'col_1'=4] {'row_0','row_1'..., dimensions={0} | all-to-all | bytes 40960 | tf_op jit(solution)/shard_map/all_to_all | solution.py:152
  610.2 5.5 collective-permute-start.73
  617.6 5.4 collective-permute-done.72
  (483 shorter events, 361.2 us)
Async XLA Ops:
  13.6 27.3 %collective-permute-start.3 = (f32[2,160]{1,0:T(2,128)S(1)}, f32[2,160]{1,0:T(2,128)S(1)}, u32[]{:S(2)}, u32[]{:S(2)}) collective-permute-start(f32[2,160]{1,0:T(2,128)S(1)} %pad_maximum_fusion.122), channel_id=1, source_target_pairs={{0,1},{1,2},{2,3},{3,4},{4,5},{5,6},{6,7},{7,8},{8,9},{9,10},{10,1... | collective-permute-start | bytes 3848 | tf_op jit(solution)/shard_map/ppermute | solution.py:67
  41.6 19.6 %collective-permute-start.4 = (f32[1,512]{1,0:T(1,128)S(1)}, f32[1,512]{1,0:T(1,128)S(1)}, u32[]{:S(2)}, u32[]{:S(2)}) collective-permute-start(f32[1,512]{1,0:T(1,128)S(1)} %get-tuple-element.45), channel_id=1, source_target_pairs={{16,0},{32,16},{48,32},{64,48},{80,64},{96,80},{112,96},{128,112},... | collective-permute-start | bytes 6152 | tf_op jit(solution)/shard_map/ppermute | solution.py:34
  43.5 17.7 %collective-permute-start.5 = (f32[1,512]{1,0:T(1,128)S(1)}, f32[1,512]{1,0:T(1,128)S(1)}, u32[]{:S(2)}, u32[]{:S(2)}) collective-permute-start(f32[1,512]{1,0:T(1,128)S(1)} %get-tuple-element.44), channel_id=1, source_target_pairs={{0,16},{16,32},{32,48},{48,64},{64,80},{80,96},{96,112},{112,128},... | collective-permute-start | bytes 6152 | tf_op jit(solution)/shard_map/ppermute | solution.py:33
  92.8 16.8 %collective-permute-start.8 = (f32[1,256]{1,0:T(1,128)S(1)}, f32[1,256]{1,0:T(1,128)S(1)}, u32[]{:S(2)}, u32[]{:S(2)}) collective-permute-start(f32[1,256]{1,0:T(1,128)S(1)} %get-tuple-element.67), channel_id=1, source_target_pairs={{16,0},{32,16},{48,32},{64,48},{80,64},{96,80},{112,96},{128,112},... | collective-permute-start | bytes 3080 | tf_op jit(solution)/shard_map/ppermute | solution.py:34
  94.7 14.8 %collective-permute-start.9 = (f32[1,256]{1,0:T(1,128)S(1)}, f32[1,256]{1,0:T(1,128)S(1)}, u32[]{:S(2)}, u32[]{:S(2)}) collective-permute-start(f32[1,256]{1,0:T(1,128)S(1)} %get-tuple-element.66), channel_id=1, source_target_pairs={{0,16},{16,32},{32,48},{48,64},{64,80},{80,96},{96,112},{112,128},... | collective-permute-start | bytes 3080 | tf_op jit(solution)/shard_map/ppermute | solution.py:33
  120.0 15.6 %collective-permute-start.12 = (f32[1,128]{1,0:T(1,128)S(1)}, f32[1,128]{1,0:T(1,128)S(1)}, u32[]{:S(2)}, u32[]{:S(2)}) collective-permute-start(f32[1,128]{1,0:T(1,128)S(1)} %get-tuple-element.89), channel_id=1, source_target_pairs={{16,0},{32,16},{48,32},{64,48},{80,64},{96,80},{112,96},{128,112},... | collective-permute-start | bytes 1544 | tf_op jit(solution)/shard_map/ppermute | solution.py:34
  121.9 13.7 %collective-permute-start.13 = (f32[1,128]{1,0:T(1,128)S(1)}, f32[1,128]{1,0:T(1,128)S(1)}, u32[]{:S(2)}, u32[]{:S(2)}) collective-permute-start(f32[1,128]{1,0:T(1,128)S(1)} %get-tuple-element.88), channel_id=1, source_target_pairs={{0,16},{16,32},{32,48},{48,64},{64,80},{80,96},{96,112},{112,128},... | collective-permute-start | bytes 1544 | tf_op jit(solution)/shard_map/ppermute | solution.py:33
  157.2 38.3 %all-to-all-start = ((f32[16,1,320]{2,1,0:T(1,128)}), f32[16,1,320]{2,1,0:T(1,128)S(1)}, u32[]{:S(2)}, u32[]{:S(2)}) async-start(f32[16,1,320]{2,1,0:T(1,128)} %reshape.213), calls=%async_computation | async-start | bytes 49152 | tf_op jit(solution)/shard_map/all_to_all | solution.py:57
  204.0 18.7 %all-to-all-start.1 = ((f32[16,1,320]{2,1,0:T(1,128)}), f32[16,1,320]{2,1,0:T(1,128)S(1)}, u32[]{:S(2)}, u32[]{:S(2)}) async-start(f32[16,1,320]{2,1,0:T(1,128)} %reshape.215), calls=%async_computation.1 | async-start | bytes 49152 | tf_op jit(solution)/shard_map/all_to_all | solution.py:144
  261.6 17.0 %collective-permute-start.24 = (f32[1,128]{1,0:T(1,128)S(1)}, f32[1,128]{1,0:T(1,128)S(1)}, u32[]{:S(2)}, u32[]{:S(2)}) collective-permute-start(f32[1,128]{1,0:T(1,128)S(1)} %get-tuple-element.85), channel_id=1, source_target_pairs={{16,0},{32,16},{48,32},{64,48},{80,64},{96,80},{112,96},{128,112},... | collective-permute-start | bytes 1544 | tf_op jit(solution)/shard_map/ppermute | solution.py:34
  263.6 15.0 %collective-permute-start.25 = (f32[1,128]{1,0:T(1,128)S(1)}, f32[1,128]{1,0:T(1,128)S(1)}, u32[]{:S(2)}, u32[]{:S(2)}) collective-permute-start(f32[1,128]{1,0:T(1,128)S(1)} %get-tuple-element.84), channel_id=1, source_target_pairs={{0,16},{16,32},{32,48},{48,64},{64,80},{80,96},{96,112},{112,128},... | collective-permute-start | bytes 1544 | tf_op jit(solution)/shard_map/ppermute | solution.py:33
  279.0 16.6 %collective-permute-start.28 = (f32[1,256]{1,0:T(1,128)S(1)}, f32[1,256]{1,0:T(1,128)S(1)}, u32[]{:S(2)}, u32[]{:S(2)}) collective-permute-start(f32[1,256]{1,0:T(1,128)S(1)} %get-tuple-element.63), channel_id=1, source_target_pairs={{16,0},{32,16},{48,32},{64,48},{80,64},{96,80},{112,96},{128,112},... | collective-permute-start | bytes 3080 | tf_op jit(solution)/shard_map/ppermute | solution.py:34
  280.9 14.7 %collective-permute-start.29 = (f32[1,256]{1,0:T(1,128)S(1)}, f32[1,256]{1,0:T(1,128)S(1)}, u32[]{:S(2)}, u32[]{:S(2)}) collective-permute-start(f32[1,256]{1,0:T(1,128)S(1)} %get-tuple-element.62), channel_id=1, source_target_pairs={{0,16},{16,32},{32,48},{48,64},{64,80},{80,96},{96,112},{112,128},... | collective-permute-start | bytes 3080 | tf_op jit(solution)/shard_map/ppermute | solution.py:33
  297.0 17.8 %collective-permute-start.32 = (f32[1,512]{1,0:T(1,128)S(1)}, f32[1,512]{1,0:T(1,128)S(1)}, u32[]{:S(2)}, u32[]{:S(2)}) collective-permute-start(f32[1,512]{1,0:T(1,128)S(1)} %get-tuple-element.41), channel_id=1, source_target_pairs={{16,0},{32,16},{48,32},{64,48},{80,64},{96,80},{112,96},{128,112},... | collective-permute-start | bytes 6152 | tf_op jit(solution)/shard_map/ppermute | solution.py:34
  298.9 15.8 %collective-permute-start.33 = (f32[1,512]{1,0:T(1,128)S(1)}, f32[1,512]{1,0:T(1,128)S(1)}, u32[]{:S(2)}, u32[]{:S(2)}) collective-permute-start(f32[1,512]{1,0:T(1,128)S(1)} %get-tuple-element.40), channel_id=1, source_target_pairs={{0,16},{16,32},{32,48},{48,64},{64,80},{80,96},{96,112},{112,128},... | collective-permute-start | bytes 6152 | tf_op jit(solution)/shard_map/ppermute | solution.py:33
  315.1 13.8 %collective-permute-start.36 = (f32[1,512]{1,0:T(1,128)S(1)}, f32[1,512]{1,0:T(1,128)S(1)}, u32[]{:S(2)}, u32[]{:S(2)}) collective-permute-start(f32[1,512]{1,0:T(1,128)S(1)} %get-tuple-element.37), channel_id=1, source_target_pairs={{16,0},{32,16},{48,32},{64,48},{80,64},{96,80},{112,96},{128,112},... | collective-permute-start | bytes 6152 | tf_op jit(solution)/shard_map/ppermute | solution.py:34
  323.0 32.6 %collective-permute-start.41 = (f32[160,1]{1,0:T(8,128)S(1)}, f32[160,1]{1,0:T(8,128)S(1)}, u32[]{:S(2)}, u32[]{:S(2)}) collective-permute-start(f32[160,1]{1,0:T(8,128)S(1)} %get-tuple-element.35), channel_id=1, source_target_pairs={{0,1},{1,2},{2,3},{3,4},{4,5},{5,6},{6,7},{7,8},{8,9},{9,10},{10,1... | collective-permute-start | bytes 1928 | tf_op jit(solution)/shard_map/ppermute | solution.py:33
  330.6 24.3 %collective-permute-start.40 = (f32[2,160]{1,0:T(2,128)S(1)}, f32[2,160]{1,0:T(2,128)S(1)}, u32[]{:S(2)}, u32[]{:S(2)}) collective-permute-start(f32[2,160]{1,0:T(2,128)S(1)} %pad_maximum_fusion.123), channel_id=1, source_target_pairs={{0,1},{1,2},{2,3},{3,4},{4,5},{5,6},{6,7},{7,8},{8,9},{9,10},{10,1... | collective-permute-start | bytes 3848 | tf_op jit(solution)/shard_map/ppermute | solution.py:67
  358.0 16.1 %collective-permute-start.42 = (f32[1,512]{1,0:T(1,128)S(1)}, f32[1,512]{1,0:T(1,128)S(1)}, u32[]{:S(2)}, u32[]{:S(2)}) collective-permute-start(f32[1,512]{1,0:T(1,128)S(1)} %get-tuple-element.33), channel_id=1, source_target_pairs={{16,0},{32,16},{48,32},{64,48},{80,64},{96,80},{112,96},{128,112},... | collective-permute-start | bytes 6152 | tf_op jit(solution)/shard_map/ppermute | solution.py:34
  359.9 14.2 %collective-permute-start.43 = (f32[1,512]{1,0:T(1,128)S(1)}, f32[1,512]{1,0:T(1,128)S(1)}, u32[]{:S(2)}, u32[]{:S(2)}) collective-permute-start(f32[1,512]{1,0:T(1,128)S(1)} %get-tuple-element.32), channel_id=1, source_target_pairs={{0,16},{16,32},{32,48},{48,64},{64,80},{80,96},{96,112},{112,128},... | collective-permute-start | bytes 6152 | tf_op jit(solution)/shard_map/ppermute | solution.py:33
  405.6 17.4 %collective-permute-start.46 = (f32[1,256]{1,0:T(1,128)S(1)}, f32[1,256]{1,0:T(1,128)S(1)}, u32[]{:S(2)}, u32[]{:S(2)}) collective-permute-start(f32[1,256]{1,0:T(1,128)S(1)} %get-tuple-element.59), channel_id=1, source_target_pairs={{16,0},{32,16},{48,32},{64,48},{80,64},{96,80},{112,96},{128,112},... | collective-permute-start | bytes 3080 | tf_op jit(solution)/shard_map/ppermute | solution.py:34
  407.6 15.5 %collective-permute-start.47 = (f32[1,256]{1,0:T(1,128)S(1)}, f32[1,256]{1,0:T(1,128)S(1)}, u32[]{:S(2)}, u32[]{:S(2)}) collective-permute-start(f32[1,256]{1,0:T(1,128)S(1)} %get-tuple-element.58), channel_id=1, source_target_pairs={{0,16},{16,32},{32,48},{48,64},{64,80},{80,96},{96,112},{112,128},... | collective-permute-start | bytes 3080 | tf_op jit(solution)/shard_map/ppermute | solution.py:33
  433.5 15.6 %collective-permute-start.50 = (f32[1,128]{1,0:T(1,128)S(1)}, f32[1,128]{1,0:T(1,128)S(1)}, u32[]{:S(2)}, u32[]{:S(2)}) collective-permute-start(f32[1,128]{1,0:T(1,128)S(1)} %get-tuple-element.81), channel_id=1, source_target_pairs={{16,0},{32,16},{48,32},{64,48},{80,64},{96,80},{112,96},{128,112},... | collective-permute-start | bytes 1544 | tf_op jit(solution)/shard_map/ppermute | solution.py:34
  435.5 13.7 %collective-permute-start.51 = (f32[1,128]{1,0:T(1,128)S(1)}, f32[1,128]{1,0:T(1,128)S(1)}, u32[]{:S(2)}, u32[]{:S(2)}) collective-permute-start(f32[1,128]{1,0:T(1,128)S(1)} %get-tuple-element.80), channel_id=1, source_target_pairs={{0,16},{16,32},{32,48},{48,64},{64,80},{80,96},{96,112},{112,128},... | collective-permute-start | bytes 1544 | tf_op jit(solution)/shard_map/ppermute | solution.py:33
  469.4 13.6 %all-to-all-start.3 = ((f32[16,1,320]{2,1,0:T(1,128)}), f32[16,1,320]{2,1,0:T(1,128)S(1)}, u32[]{:S(2)}, u32[]{:S(2)}) async-start(f32[16,1,320]{2,1,0:T(1,128)} %reshape.219), calls=%async_computation.3 | async-start | bytes 49152 | tf_op jit(solution)/shard_map/all_to_all | solution.py:57
  490.4 42.5 %all-to-all-start.4 = ((f32[16,1,320]{2,1,0:T(1,128)}), f32[16,1,320]{2,1,0:T(1,128)S(1)}, u32[]{:S(2)}, u32[]{:S(2)}) async-start(f32[16,1,320]{2,1,0:T(1,128)} %reshape.221), calls=%async_computation.4 | async-start | bytes 49152 | tf_op jit(solution)/shard_map/all_to_all | solution.py:144
  569.9 16.6 %collective-permute-start.62 = (f32[1,128]{1,0:T(1,128)S(1)}, f32[1,128]{1,0:T(1,128)S(1)}, u32[]{:S(2)}, u32[]{:S(2)}) collective-permute-start(f32[1,128]{1,0:T(1,128)S(1)} %get-tuple-element.77), channel_id=1, source_target_pairs={{16,0},{32,16},{48,32},{64,48},{80,64},{96,80},{112,96},{128,112},... | collective-permute-start | bytes 1544 | tf_op jit(solution)/shard_map/ppermute | solution.py:34
  571.8 14.7 %collective-permute-start.63 = (f32[1,128]{1,0:T(1,128)S(1)}, f32[1,128]{1,0:T(1,128)S(1)}, u32[]{:S(2)}, u32[]{:S(2)}) collective-permute-start(f32[1,128]{1,0:T(1,128)S(1)} %get-tuple-element.76), channel_id=1, source_target_pairs={{0,16},{16,32},{32,48},{48,64},{64,80},{80,96},{96,112},{112,128},... | collective-permute-start | bytes 1544 | tf_op jit(solution)/shard_map/ppermute | solution.py:33
  586.9 15.4 %collective-permute-start.66 = (f32[1,256]{1,0:T(1,128)S(1)}, f32[1,256]{1,0:T(1,128)S(1)}, u32[]{:S(2)}, u32[]{:S(2)}) collective-permute-start(f32[1,256]{1,0:T(1,128)S(1)} %get-tuple-element.55), channel_id=1, source_target_pairs={{16,0},{32,16},{48,32},{64,48},{80,64},{96,80},{112,96},{128,112},... | collective-permute-start | bytes 3080 | tf_op jit(solution)/shard_map/ppermute | solution.py:34
  588.8 13.5 %collective-permute-start.67 = (f32[1,256]{1,0:T(1,128)S(1)}, f32[1,256]{1,0:T(1,128)S(1)}, u32[]{:S(2)}, u32[]{:S(2)}) collective-permute-start(f32[1,256]{1,0:T(1,128)S(1)} %get-tuple-element.54), channel_id=1, source_target_pairs={{0,16},{16,32},{32,48},{48,64},{64,80},{80,96},{96,112},{112,128},... | collective-permute-start | bytes 3080 | tf_op jit(solution)/shard_map/ppermute | solution.py:33
  603.6 19.4 %collective-permute-start.70 = (f32[1,512]{1,0:T(1,128)S(1)}, f32[1,512]{1,0:T(1,128)S(1)}, u32[]{:S(2)}, u32[]{:S(2)}) collective-permute-start(f32[1,512]{1,0:T(1,128)S(1)} %get-tuple-element.29), channel_id=1, source_target_pairs={{16,0},{32,16},{48,32},{64,48},{80,64},{96,80},{112,96},{128,112},... | collective-permute-start | bytes 6152 | tf_op jit(solution)/shard_map/ppermute | solution.py:34
  605.5 17.5 %collective-permute-start.71 = (f32[1,512]{1,0:T(1,128)S(1)}, f32[1,512]{1,0:T(1,128)S(1)}, u32[]{:S(2)}, u32[]{:S(2)}) collective-permute-start(f32[1,512]{1,0:T(1,128)S(1)} %get-tuple-element.28), channel_id=1, source_target_pairs={{0,16},{16,32},{32,48},{48,64},{64,80},{80,96},{96,112},{112,128},... | collective-permute-start | bytes 6152 | tf_op jit(solution)/shard_map/ppermute | solution.py:33
  (73 other events, 2494.7 us)
where the time goes:
time: 637 us; the launch traced here: 625 us
  starting transfers between devices  257 us (40%)
  local copies, waits for them, and re-layouts  110 us (17%)
  waiting for transfers between devices  88.3 us (14%)
  blocking collectives  86.8 us (14%)
  other arithmetic  49 us (8%)
  matrix products  26.7 us (4%)
  between operations  6.4 us (1%)
    ppermute x34, starting transfers between devices, with_halo(): lax.ppermute(last, axis, up)  145 us
    psum x10, blocking collectives, over_axes(): return functools.reduce(lax.psum, axes, x)  74.4 us
    ppermute x34, waiting for transfers between devices, with_halo(): lax.ppermute(leading, axis, [(b, a) for a, b in up])  73 us
    reshape x8, local copies, waits for them, and re-layouts, cycle(): residual.reshape(rows // 2, 2, cols // 2, 2).sum(axis=(1, 3))  61.4 us
    ppermute x34, starting transfers between devices, with_halo(): lax.ppermute(leading, axis, [(b, a) for a, b in up])  56.5 us
    reduce_sum x8, other arithmetic, cycle(): residual.reshape(rows // 2, 2, cols // 2, 2).sum(axis=(1, 3))  25.4 us
    ppermute x6, starting transfers between devices, from_behind(): lax.ppermute(value, axis, [(source, source + steps) for source in range(l...  23.2 us
    slice x16, local copies, waits for them, and re-layouts, coarse_weights(): rightward = w_right[0::2, 1::2] + w_right[1::2, 1::2]  17.5 us
  transfers between devices with their start and end apart: 79, of which 23 were waited for; matrix products, arithmetic and copies ran while one was open for 8% of the time, Pallas kernels for 0%

commit v1 on v0

v1 whole, which is shorter than its diff:
```python
import functools

import jax
import jax.numpy as jnp
import numpy as np
from jax import lax
from jax.experimental import pallas as pl
from jax.experimental.pallas import tpu as pltpu
from jax.sharding import PartitionSpec as P

MESH = pl.DeviceIdType.MESH
HIGHEST = lax.Precision.HIGHEST
F32 = jnp.float32

GRIDS = 4
NCLASS = 8
LEVELS = 256
DAMPING = 0.8
DIAG_FLOOR = 0.5
TURN = 2.0 * np.pi
ERROR_FLOOR = 0.5
EPSILON = 1e-6
SCREEN_WIDTH = 4.0

STEP = 2**GRIDS
HALO = 48
ROWS = 160
COLS = 512
CROWS = ROWS // STEP
CCOLS = COLS // STEP
EXT = ROWS + 2 * HALO
SUB = EXT // STEP
OWN_CHUNKS = COLS // 128
CHUNKS = OWN_CHUNKS + 1
WIDTH = CHUNKS * 128
FREQ = 256
PAD = 48
SHIFTS = (1, 2, 4, 8, 16, 32)
HALVES = tuple(slice(h, h + 8) for h in range(0, SUB, 8))


def tables(rows, cols):
    devices = rows // CROWS
    freq = np.arange(rows)[:, None]
    cosine = np.cos(np.pi * (np.arange(rows)[None, :] + 0.5) * freq / rows) * np.sqrt(2.0 / rows)
    cosine[0] *= np.sqrt(0.5)
    forward = np.zeros((2, devices, 8, FREQ))
    backward = np.zeros((devices, SUB, FREQ))
    for d in range(devices):
        for k in range(CROWS):
            forward[k // 8, d, k % 8, :rows] = cosine[:, d * CROWS + k]
        for k in range(SUB):
            place = d * CROWS + (k if k < CROWS + HALO // STEP else k - SUB)
            if 0 <= place < rows:
                backward[d, k, :rows] = cosine[:, place]
    shift = 2.0 - 2.0 * np.cos(np.pi * np.arange(rows) / rows) + (SCREEN_WIDTH / cols) ** 2
    theta = 2.0 * np.arcsinh(np.sqrt(shift) / 2.0)
    constants = np.zeros((16, FREQ))
    constants[0] = 1.0
    constants[0, :rows] = theta
    constants[1, :rows] = 1.0 / (2.0 * np.sinh(theta))
    constants[2] = 1.0
    constants[2, :rows] = 1.0 / (1.0 - np.exp(-2.0 * cols * theta))
    for i, s in enumerate(SHIFTS):
        constants[3 + i] = np.exp(-s * constants[0])
    return (
        forward.reshape(2, devices * 8, FREQ).astype(np.float32),
        backward.astype(np.float32),
        constants.astype(np.float32),
    )


def ahead(x, s):
    return pltpu.roll(x, WIDTH - s, 1)


def behind(x, s):
    return pltpu.roll(x, s, 1)


def wrap(ref, above=True, below=True):
    last = ref.shape[0] - 2
    if above:
        ref[0] = pltpu.roll(ref[last], 1, 0)
    if below:
        ref[last + 1] = pltpu.roll(ref[1], SUB - 1, 0)


def steps(count, body):
    if count <= 2:
        for i in range(count):
            body(i)
    else:

        def step(i, carry):
            body(i)
            return carry

        lax.fori_loop(0, count, step, 0)


def kernel(R, C, *refs):
    (
        swath_h,
        coherence_h,
        counts_h,
        forward_h,
        backward_h,
        constants_h,
        out_h,
        swath,
        coherence,
        counts,
        forward,
        backward,
        constants,
        nat,
        left_pack,
        right_pack,
        from_left,
        from_right,
        result,
        qual,
        phase,
        wd,
        wr,
        sd,
        sr,
        v0,
        rdiv0,
        first,
        gd,
        gr,
        *rest,
    ) = refs
    levels = []
    for _ in range(3):
        levels.append(rest[:6])
        rest = rest[6:]
    (
        coarse,
        select,
        spread,
        blocks,
        amps,
        near_send,
        near_left,
        near_right,
        ext,
        powers,
        coef,
        load_sem,
        p1_send,
        p1_recv,
        p2_send,
        p2_recv,
        p3_send,
        p3_recv,
        nb_send,
        nb_recv,
        out_sem,
    ) = rest

    r = lax.axis_index("row")
    c = lax.axis_index("col")
    N = CCOLS * C

    loads = [
        pltpu.make_async_copy(swath_h, swath, load_sem.at[0]),
        pltpu.make_async_copy(coherence_h, coherence, load_sem.at[1]),
        pltpu.make_async_copy(counts_h, counts, load_sem.at[2]),
        pltpu.make_async_copy(constants_h, constants, load_sem.at[3]),
        pltpu.make_async_copy(forward_h, forward, load_sem.at[4]),
        pltpu.make_async_copy(backward_h.at[r], backward, load_sem.at[5]),
    ]
    for copy in loads:
        copy.start()

    for a in range(2):
        for k in range(OWN_CHUNKS):
            nat[a, k, ROWS:EXT, :] = jnp.zeros((EXT - ROWS, 128), F32)
    from_left[...] = jnp.zeros((EXT, 128), F32)
    from_right[...] = jnp.zeros((EXT, 128), F32)
    near_left[...] = jnp.zeros(near_left.shape, F32)
    near_right[...] = jnp.zeros(near_right.shape, F32)

    barrier = pltpu.get_barrier_semaphore()
    for i in range(1, R):
        pl.semaphore_signal(barrier, inc=1, device_id=(lax.rem(r + i, R), c), device_id_type=MESH)
    for i in range(1, C):
        pl.semaphore_signal(barrier, inc=1, device_id=(r, lax.rem(c + i, C)), device_id_type=MESH)
    for i in (1, R - 1):
        for j in (1, C - 1):
            pl.semaphore_signal(
                barrier, inc=1, device_id=(lax.rem(r + i, R), lax.rem(c + j, C)), device_id_type=MESH
            )

    for copy in loads[:3]:
        copy.wait()
    lane = lax.broadcasted_iota(jnp.int32, (32, 128), 1)

    def prepare(i):
        rows = pl.ds(pl.multiple_of(i * 32, 32), 32)
        for k in range(OWN_CHUNKS):
            span = slice(128 * k, 128 * k + 128)
            level = coherence[rows, span].astype(F32) * (1.0 / (NCLASS - 1))
            q = swath[rows, span].astype(F32) * (level * level)
            ph = counts[rows, span].astype(F32) * (1.0 / LEVELS)
            nat[0, k, rows, :] = q
            nat[1, k, rows, :] = ph
            if k == 0:
                left_pack[rows, :] = jnp.where(lane < 64, q, pltpu.roll(ph, 64, 1))
            if k == OWN_CHUNKS - 1:
                right_pack[rows, :] = jnp.where(lane < 64, pltpu.roll(ph, 64, 1), q)

    steps(ROWS // 32, prepare)
    pl.semaphore_wait(barrier, R + C + 2)

    top, bottom = slice(0, HALO), slice(ROWS - HALO, ROWS)
    own, below, above = slice(0, ROWS), slice(ROWS, ROWS + HALO), slice(ROWS + HALO, EXT)
    chunks = slice(0, OWN_CHUNKS)
    is_up, is_down = r > 0, r < R - 1
    is_left, is_right = c > 0, c < C - 1
    both = jnp.logical_and
    plan = [
        (is_up, -1, 0, nat.at[:, chunks, top, :], nat.at[:, chunks, below, :], is_down),
        (is_down, 1, 0, nat.at[:, chunks, bottom, :], nat.at[:, chunks, above, :], is_up),
        (is_left, 0, -1, left_pack, from_right.at[own], is_right),
        (is_right, 0, 1, right_pack, from_left.at[own], is_left),
        (both(is_up, is_left), -1, -1, left_pack.at[top], from_right.at[below], both(is_down, is_right)),
        (both(is_down, is_left), 1, -1, left_pack.at[bottom], from_right.at[above], both(is_up, is_right)),
        (both(is_up, is_right), -1, 1, right_pack.at[top], from_left.at[below], both(is_down, is_left)),
        (both(is_down, is_right), 1, 1, right_pack.at[bottom], from_left.at[above], both(is_up, is_left)),
    ]
    halo_copies = []
    for i, (sends, dr, dc, source, target, receives) in enumerate(plan):
        copy = pltpu.make_async_remote_copy(
            src_ref=source,
            dst_ref=target,
            send_sem=p1_send.at[i],
            recv_sem=p1_recv.at[i],
            device_id=(lax.rem(r + dr + R, R), lax.rem(c + dc + C, C)),
            device_id_type=MESH,
        )
        halo_copies.append((sends, receives, copy))
        pl.when(sends)(copy.start)

    for copy in loads[3:]:
        copy.wait()
    theta = constants[0:1, :]
    green = constants[1:2, :]
    inverse = constants[2:3, :]
    yy = lax.broadcasted_iota(jnp.int32, (CCOLS, FREQ), 0)
    last = CCOLS - 1
    powers[0] = jnp.exp(-theta * (last - yy).astype(F32))
    powers[1] = jnp.exp(-theta * yy.astype(F32))
    powers[2] = jnp.where(yy <= last - 3, jnp.exp(-theta * jnp.maximum(last - 3 - yy, 0).astype(F32)), 0.0)
    powers[3] = jnp.where(yy >= 3, jnp.exp(-theta * jnp.maximum(yy - 3, 0).astype(F32)), 0.0)

    def decay(n):
        return jnp.exp(-theta * n.astype(F32))

    def directly(n, inside):
        return jnp.where(inside, decay(jnp.maximum(n, 0)), 0.0)

    for i in range(C):
        rev = C - 1 - i
        coef[0, i, 0:1, :] = directly(CCOLS * (c - 1 - i) - 3, i < c - 1) + inverse * decay(
            N + CCOLS * rev + CCOLS * c - 3
        )
        coef[0, i, 1:2, :] = inverse * decay(CCOLS * i + CCOLS * c - 3)
        coef[1, i, 0:1, :] = inverse * decay(CCOLS * (C - 1 - c) + CCOLS * rev - 3)
        coef[1, i, 1:2, :] = directly(CCOLS * (i - c - 1) - 3, i > c + 1) + inverse * decay(
            2 * N - CCOLS * (c + 1) + CCOLS * i - 3
        )
    at = lax.broadcasted_iota(jnp.int32, (COLS, 128), 0)
    to = lax.broadcasted_iota(jnp.int32, (COLS, 128), 1)
    select[...] = jnp.where((to < 64) & (at == STEP * (to & 31)), 1.0, 0.0).astype(F32)
    at = lax.broadcasted_iota(jnp.int32, (PAD, WIDTH), 0)
    to = lax.broadcasted_iota(jnp.int32, (PAD, WIDTH), 1) >> GRIDS
    spread[...] = jnp.where(at == jnp.where(to < CCOLS + 3, to + 8, to + 8 - WIDTH // STEP), 1.0, 0.0).astype(F32)
    ext[...] = jnp.zeros((PAD, FREQ), F32)

    for _, receives, copy in halo_copies:
        pl.when(receives)(copy.wait_recv)

    lane = lax.broadcasted_iota(jnp.int32, (SUB, 128), 1)
    for p in range(STEP):
        rows = pl.ds(p, SUB, stride=STEP)
        for k in range(OWN_CHUNKS):
            span = slice(128 * k, 128 * k + 128)
            qual[p + 1, :, span] = nat.at[0, k][rows, :]
            phase[p + 1, :, span] = nat.at[1, k][rows, :]
        a, b = from_right[rows, :], from_left[rows, :]
        qual[p + 1, :, COLS:WIDTH] = jnp.where(lane < 64, a, b)
        phase[p + 1, :, COLS:WIDTH] = pltpu.roll(jnp.where(lane < 64, b, a), 64, 1)
    wrap(qual, above=False)
    wrap(phase, above=False)

    def steep(u):
        return u - jnp.floor(u + 0.5)

    def make_faces(p):
        for h in HALVES:
            q, ph = qual[p + 1, h], phase[p + 1, h]
            wd[p + 1, h] = jnp.minimum(q, qual[p + 2, h])
            wr[p, h] = jnp.minimum(q, ahead(q, 1))
            sd[p + 1, h] = steep(phase[p + 2, h] - ph)
            sr[p, h] = steep(ahead(ph, 1) - ph)

    steps(STEP, make_faces)
    wrap(wd, below=False)
    wrap(sd, below=False)

    def start_first(p):
        for h in HALVES:
            a, au, b = wd[p + 1, h], wd[p, h], wr[p, h]
            fr = b * sr[p, h]
            source = au * sd[p, h] - a * sd[p + 1, h] + behind(fr, 1) - fr
            rdiv = DAMPING / jnp.maximum(a + au + b + behind(b, 1), DIAG_FLOOR)
            rdiv0[p, h] = rdiv
            v0[p + 1, h] = source * rdiv

    steps(STEP, start_first)
    wrap(v0)

    def restrict_fine():
        src, a1, b1 = levels[0][0], levels[0][1], levels[0][2]

        def body(i):
            for h in HALVES:
                va, v1, v2, vb = v0[2 * i, h], v0[2 * i + 1, h], v0[2 * i + 2, h], v0[2 * i + 3, h]
                a_odd = wd[2 * i + 2, h]
                y = a_odd * (vb - v2 - sd[2 * i + 2, h]) - wd[2 * i, h] * (v1 - va - sd[2 * i, h])
                b0, b_odd = wr[2 * i, h], wr[2 * i + 1, h]
                g = b0 * (ahead(v1, 1) - v1 - sr[2 * i, h]) + b_odd * (ahead(v2, 1) - v2 - sr[2 * i + 1, h])
                src[i, h] = y + ahead(y + g, 1) - behind(g, 1)
                a1[i + 1, h] = a_odd + ahead(a_odd, 1)
                b1[i, h] = ahead(b0 + b_odd, 1)

        steps(STEP // 2, body)
        wrap(a1, below=False)

    def down(level):
        s = 2**level
        count = STEP // s
        src, a, b, rdiv, v, _ = levels[level - 1]

        def smooth(p):
            for h in HALVES:
                bb = b[p, h]
                d = DAMPING / jnp.maximum(a[p + 1, h] + a[p, h] + bb + behind(bb, s), DIAG_FLOOR)
                rdiv[p, h] = d
                v[p + 1, h] = src[p, h] * d

        steps(count, smooth)
        wrap(v)
        if level < GRIDS - 1:
            src_n, a_n, b_n = levels[level][0], levels[level][1], levels[level][2]
        else:
            src_n, a_n, b_n = None, None, None

        def body(i):
            for h in HALVES:
                va, v1, v2, vb = v[2 * i, h], v[2 * i + 1, h], v[2 * i + 2, h], v[2 * i + 3, h]
                a_odd = a[2 * i + 2, h]
                t = src[2 * i, h] + src[2 * i + 1, h] + a_odd * (vb - v2) - a[2 * i, h] * (v1 - va)
                b0, b_odd = b[2 * i, h], b[2 * i + 1, h]
                g = b0 * (ahead(v1, s) - v1) + b_odd * (ahead(v2, s) - v2)
                out = t + ahead(t + g, s) - behind(g, s)
                if src_n is None:
                    coarse[h] = out
                else:
                    src_n[i, h] = out
                    a_n[i + 1, h] = a_odd + ahead(a_odd, s)
                    b_n[i, h] = ahead(b0 + b_odd, s)

        steps(count // 2, body)
        if a_n is not None:
            wrap(a_n, below=False)

    def up(level):
        s = 2**level
        count = STEP // s
        src, a, b, rdiv, v, out = levels[level - 1]

        def add(i):
            for h in HALVES:
                if level == GRIDS - 1:
                    x = coarse[h]
                else:
                    x = levels[level][5][i, h]
                    column = lax.broadcasted_iota(jnp.int32, x.shape, 1)
                    x = jnp.where((column & s) == 0, x, behind(x, s))
                v[2 * i + 1, h] = v[2 * i + 1, h] + x
                v[2 * i + 2, h] = v[2 * i + 2, h] + x

        steps(count // 2, add)
        wrap(v)

        def smooth(i):
            for h in HALVES:
                va, v1, v2, vb = v[2 * i, h], v[2 * i + 1, h], v[2 * i + 2, h], v[2 * i + 3, h]
                g0 = a[2 * i, h] * (v1 - va)
                g1 = a[2 * i + 1, h] * (v2 - v1)
                g2 = a[2 * i + 2, h] * (vb - v2)
                f1 = b[2 * i, h] * (ahead(v1, s) - v1)
                f2 = b[2 * i + 1, h] * (ahead(v2, s) - v2)
                out[2 * i, h] = v1 + (src[2 * i, h] + g1 - g0 + f1 - behind(f1, s)) * rdiv[2 * i, h]
                out[2 * i + 1, h] = v2 + (src[2 * i + 1, h] + g2 - g1 + f2 - behind(f2, s)) * rdiv[2 * i + 1, h]

        steps(count // 2, smooth)

    def up_fine():
        def add(i):
            for h in HALVES:
                x = levels[0][5][i, h]
                column = lax.broadcasted_iota(jnp.int32, x.shape, 1)
                x = jnp.where((column & 1) == 0, x, behind(x, 1))
                v0[2 * i + 1, h] = v0[2 * i + 1, h] + x
                v0[2 * i + 2, h] = v0[2 * i + 2, h] + x

        steps(STEP // 2, add)
        wrap(v0)

        def smooth(i):
            for h in HALVES:
                va, v1, v2, vb = v0[2 * i, h], v0[2 * i + 1, h], v0[2 * i + 2, h], v0[2 * i + 3, h]
                g0 = wd[2 * i, h] * (v1 - va - sd[2 * i, h])
                g1 = wd[2 * i + 1, h] * (v2 - v1 - sd[2 * i + 1, h])
                g2 = wd[2 * i + 2, h] * (vb - v2 - sd[2 * i + 2, h])
                f1 = wr[2 * i, h] * (ahead(v1, 1) - v1 - sr[2 * i, h])
                f2 = wr[2 * i + 1, h] * (ahead(v2, 1) - v2 - sr[2 * i + 1, h])
                first[2 * i + 1, h] = v1 + (g1 - g0 + f1 - behind(f1, 1)) * rdiv0[2 * i, h]
                first[2 * i + 2, h] = v2 + (g2 - g1 + f2 - behind(f2, 1)) * rdiv0[2 * i + 1, h]

        steps(STEP // 2, smooth)

    def coarse_solve(turn):
        _, a3, b3, _, _, _ = levels[2]
        column = lax.broadcasted_iota(jnp.int32, (SUB, COLS), 1)
        line = lax.broadcasted_iota(jnp.int32, (SUB, COLS), 0)
        here = slice(0, COLS)
        part = jnp.where((column & 7) == 0, a3[2, :, here], 0.0) + jnp.where(
            (column & 15) == 8, b3[0, :, here] + b3[1, :, here], 0.0
        )
        part = jnp.where((line < CROWS) & ((column & 7) == 0), part, 0.0)
        local = jnp.sum(jnp.sum(part, axis=1, keepdims=True), axis=0, keepdims=True)
        mine = jnp.dot(coarse[:, here], select[...], precision=HIGHEST, preferred_element_type=F32)
        spot = lax.broadcasted_iota(jnp.int32, (8, 128), 1)
        blocks[turn, r] = jnp.where(spot < 32, mine[0:8], jnp.where(spot < 64, mine[8:16], local))
        copies = []
        for i in range(1, R):
            copy = pltpu.make_async_remote_copy(
                src_ref=blocks.at[turn, r],
                dst_ref=blocks.at[turn, r],
                send_sem=p2_send.at[turn, i - 1],
                recv_sem=p2_recv.at[turn, i - 1],
                device_id=(lax.rem(r + i, R), c),
                device_id_type=MESH,
            )
            copy.start()
            copies.append(copy)
        for copy in copies:
            copy.wait_recv()
        every = blocks[turn].reshape(R * 8, 128).T
        hat = jnp.dot(every[0:32], forward[0], precision=HIGHEST, preferred_element_type=F32) + jnp.dot(
            every[32:64], forward[1], precision=HIGHEST, preferred_element_type=F32
        )
        rows_sum = jnp.sum(every[64:65], axis=1, keepdims=True) * 0.125

        def total(n):
            return jnp.sum(powers[n] * hat, axis=0, keepdims=True)

        mode = lax.broadcasted_iota(jnp.int32, (1, FREQ), 1)
        amps[turn, c, 0:1, :] = jnp.where(mode < CROWS * R, total(0), rows_sum)
        amps[turn, c, 1:2, :] = total(1)
        near_send[turn, 0, 0:1, :] = total(2)
        near_send[turn, 0, 1:4, :] = hat[CCOLS - 3 : CCOLS]
        near_send[turn, 1, 0:3, :] = hat[0:3]
        near_send[turn, 1, 3:4, :] = total(3)
        for i in range(1, C):
            copy = pltpu.make_async_remote_copy(
                src_ref=amps.at[turn, c],
                dst_ref=amps.at[turn, c],
                send_sem=p3_send.at[turn, i - 1],
                recv_sem=p3_recv.at[turn, i - 1],
                device_id=(r, lax.rem(c + i, C)),
                device_id_type=MESH,
            )
            copy.start()
            copies.append(copy)
        rightward = pltpu.make_async_remote_copy(
            src_ref=near_send.at[turn, 0],
            dst_ref=near_left.at[turn],
            send_sem=nb_send.at[turn, 0],
            recv_sem=nb_recv.at[turn, 0],
            device_id=(r, lax.rem(c + 1, C)),
            device_id_type=MESH,
        )
        leftward = pltpu.make_async_remote_copy(
            src_ref=near_send.at[turn, 1],
            dst_ref=near_right.at[turn],
            send_sem=nb_send.at[turn, 1],
            recv_sem=nb_recv.at[turn, 1],
            device_id=(r, lax.rem(c + C - 1, C)),
            device_id_type=MESH,
        )
        pl.when(is_right)(rightward.start)
        pl.when(is_left)(leftward.start)
        pl.when(is_left)(rightward.wait_recv)
        pl.when(is_right)(leftward.wait_recv)
        for copy in copies[R - 1 :]:
            copy.wait_recv()
        into_left = jnp.zeros((2, FREQ), F32)
        into_right = jnp.zeros((2, FREQ), F32)
        weight = jnp.zeros((2, FREQ), F32)
        for i in range(C):
            x = amps[turn, i]
            into_left += coef[0, i] * x
            into_right += coef[1, i] * x
            weight += x
        into_left = into_left[0:1] + into_left[1:2]
        into_right = into_right[0:1] + into_right[1:2]
        weight = jnp.sum(jnp.where(mode == FREQ - 1, weight[0:1], 0.0), axis=1, keepdims=True)
        grid_rows, grid_cols = CROWS * R, CCOLS * C
        mean = weight * (1.0 / ((grid_rows - 1) * grid_cols + grid_rows * (grid_cols - 1))) + EPSILON
        ext[4:8, :] = near_left[turn]
        ext[4:5, :] = near_left[turn, 0:1, :] + into_left
        ext[8 : 8 + CCOLS, :] = hat
        ext[8 + CCOLS : 12 + CCOLS, :] = near_right[turn]
        ext[11 + CCOLS : 12 + CCOLS, :] = near_right[turn, 3:4, :] + into_right
        hats = ext[...]
        place = lax.broadcasted_iota(jnp.int32, (PAD, FREQ), 0)
        going_right = hats
        going_left = hats
        for i, s in enumerate(SHIFTS):
            q = constants[3 + i : 4 + i, :]
            going_right += q * jnp.where(place >= s, pltpu.roll(going_right, s, 0), 0.0)
            going_left += q * jnp.where(place < PAD - s, pltpu.roll(going_left, PAD - s, 0), 0.0)
        modes = (going_right + going_left - hats) * (green / mean)
        values = lax.dot_general(
            backward[...], modes, (((1,), (1,)), ((), ())), precision=HIGHEST, preferred_element_type=F32
        )
        coarse[...] = jnp.dot(values, spread[...], precision=HIGHEST, preferred_element_type=F32)
        return copies, rightward, leftward

    def cycle(turn):
        restrict_fine()
        for level in range(1, GRIDS):
            down(level)
        sent = coarse_solve(turn)
        for level in range(GRIDS - 1, 0, -1):
            up(level)
        up_fine()
        return sent

    sent = [cycle(0)]
    wrap(first)

    def reweight(p):
        for h in HALVES:
            f = first[p + 1, h]
            e = first[p + 2, h] - f - sd[p + 1, h]
            a = wd[p + 1, h] / jnp.maximum(jnp.abs(e) * TURN, ERROR_FLOOR)
            wd[p + 1, h] = a
            gd[p + 1, h] = a * e
            e = ahead(f, 1) - f - sr[p, h]
            b = wr[p, h] / jnp.maximum(jnp.abs(e) * TURN, ERROR_FLOOR)
            wr[p, h] = b
            gr[p, h] = b * e

    steps(STEP, reweight)
    wrap(wd, below=False)
    wrap(gd, below=False)

    def start_second(p):
        for h in HALVES:
            b, f = wr[p, h], gr[p, h]
            rdiv = DAMPING / jnp.maximum(wd[p + 1, h] + wd[p, h] + b + behind(b, 1), DIAG_FLOOR)
            rdiv0[p, h] = rdiv
            v0[p + 1, h] = first[p + 1, h] + (gd[p + 1, h] - gd[p, h] + f - behind(f, 1)) * rdiv

    steps(STEP, start_second)
    wrap(v0)
    sent.append(cycle(1))

    outs = []
    for k in range(OWN_CHUNKS):
        span = slice(128 * k, 128 * k + 128)
        for p in range(STEP):
            result.at[k][pl.ds(p, SUB, stride=STEP), :] = first[p + 1, :, span] * TURN
        copy = pltpu.make_async_copy(result.at[k, own, :], out_h.at[:, span], out_sem.at[k])
        copy.start()
        outs.append(copy)
    for sends, _, copy in halo_copies:
        pl.when(sends)(copy.wait_send)
    for copies, rightward, leftward in sent:
        for copy in copies:
            copy.wait_send()
        pl.when(is_right)(rightward.wait_send)
        pl.when(is_left)(leftward.wait_send)
    for copy in outs:
        copy.wait()


def scratch(R, C):
    def field(count):
        return pltpu.VMEM((count, SUB, WIDTH), F32)

    shapes = [
        pltpu.VMEM((ROWS, COLS), jnp.int32),
        pltpu.VMEM((ROWS, COLS), jnp.int32),
        pltpu.VMEM((ROWS, COLS), jnp.int32),
        pltpu.VMEM((2, R * 8, FREQ), F32),
        pltpu.VMEM((SUB, FREQ), F32),
        pltpu.VMEM((16, FREQ), F32),
        pltpu.VMEM((2, OWN_CHUNKS, EXT, 128), F32),
        pltpu.VMEM((ROWS, 128), F32),
        pltpu.VMEM((ROWS, 128), F32),
        pltpu.VMEM((EXT, 128), F32),
        pltpu.VMEM((EXT, 128), F32),
        pltpu.VMEM((OWN_CHUNKS, EXT, 128), F32),
    ]
    padded, plain = STEP + 2, STEP
    shapes += [field(n) for n in (padded, padded, padded, plain, padded, plain, padded, plain, padded, padded, plain)]
    for level in range(1, GRIDS):
        n = STEP >> level
        shapes += [field(m) for m in (n, n + 2, n, n, n + 2, n)]
    shapes += [
        pltpu.VMEM((SUB, WIDTH), F32),
        pltpu.VMEM((COLS, 128), F32),
        pltpu.VMEM((PAD, WIDTH), F32),
        pltpu.VMEM((2, R, 8, 128), F32),
        pltpu.VMEM((2, C, 2, FREQ), F32),
        pltpu.VMEM((2, 2, 4, FREQ), F32),
        pltpu.VMEM((2, 4, FREQ), F32),
        pltpu.VMEM((2, 4, FREQ), F32),
        pltpu.VMEM((PAD, FREQ), F32),
        pltpu.VMEM((4, CCOLS, FREQ), F32),
        pltpu.VMEM((2, C, 2, FREQ), F32),
        pltpu.SemaphoreType.DMA((6,)),
        pltpu.SemaphoreType.DMA((8,)),
        pltpu.SemaphoreType.DMA((8,)),
        pltpu.SemaphoreType.DMA((2, R - 1)),
        pltpu.SemaphoreType.DMA((2, R - 1)),
        pltpu.SemaphoreType.DMA((2, C - 1)),
        pltpu.SemaphoreType.DMA((2, C - 1)),
        pltpu.SemaphoreType.DMA((2, 2)),
        pltpu.SemaphoreType.DMA((2, 2)),
        pltpu.SemaphoreType.DMA((OWN_CHUNKS,)),
    ]
    return shapes


def solution(mesh):
    R, C = mesh.shape["row"], mesh.shape["col"]
    forward, backward, constants = tables(CROWS * R, CCOLS * C)

    def body(swath, coherence, counts):
        return pl.pallas_call(
            functools.partial(kernel, R, C),
            out_shape=jax.ShapeDtypeStruct((ROWS, COLS), F32),
            in_specs=[pl.BlockSpec(memory_space=pl.ANY)] * 6,
            out_specs=pl.BlockSpec(memory_space=pl.ANY),
            scratch_shapes=scratch(R, C),
            compiler_params=pltpu.CompilerParams(
                collective_id=0, has_side_effects=True, vmem_limit_bytes=48 * 1024 * 1024
            ),
        )(swath, coherence, counts, jnp.asarray(forward), jnp.asarray(backward), jnp.asarray(constants))

    return jax.shard_map(
        body,
        mesh=mesh,
        in_specs=(P("row", "col"), P("row", "col"), P("row", "col")),
        out_specs=P("row", "col"),
        check_vma=False,
    )
```

time: 637 us -> 73.5 us (0.12)
  the two profiles are of different devices: /device:TPU:33 before, /device:TPU:1 now
where the time goes in v1:
time: 73.5 us; the launch traced here: 73.2 us
  Pallas kernels  67 us (91%)
  local copies, waits for them, and re-layouts  6.26 us (9%)
    pallas_call x1, Pallas kernels, body(): pl.pallas_call(functools.partial(kernel, R, C), out_shape=jax.ShapeDtypeS...  67 us
    unnamed x13, local copies, waits for them, and re-layouts  6.26 us

profile of v1, /device:TPU:1, one launch (start us, length us, event | category | flops | bytes accessed | tf_op | source)
XLA Modules:
  0.0 73.2 jit_solution(3020369288020048965)
XLA Ops:
  0.0 0.0 copy-start
  0.0 1.0 %copy-done = s32[160,512]{1,0:T(8,128)S(1)} copy-done((s32[160,512]{1,0:T(8,128)S(1)}, s32[160,512]{1,0:T(8,128)}, u32[]{:S(2)}) %copy-start) | copy-done | bytes 327704
  1.0 0.0 copy-start.1
  1.0 1.0 %copy-done.1 = s32[160,512]{1,0:T(8,128)S(1)} copy-done((s32[160,512]{1,0:T(8,128)S(1)}, s32[160,512]{1,0:T(8,128)}, u32[]{:S(2)}) %copy-start.1) | copy-done | bytes 327704
  1.9 0.0 copy-start.2
  1.9 1.0 %copy-done.2 = s32[160,512]{1,0:T(8,128)S(1)} copy-done((s32[160,512]{1,0:T(8,128)S(1)}, s32[160,512]{1,0:T(8,128)}, u32[]{:S(2)}) %copy-start.2) | copy-done | bytes 327704
  2.9 0.0 copy-start.3
  2.9 0.9 %copy-done.3 = f32[16,16,256]{2,1,0:T(8,128)S(1)} copy-done((f32[16,16,256]{2,1,0:T(8,128)S(1)}, f32[16,16,256]{2,1,0:T(8,128)}, u32[]{:S(2)}) %copy-start.3) | copy-done | bytes 262168
  3.9 0.0 copy-start.4
  3.9 0.9 %copy-done.4 = f32[2,128,256]{2,1,0:T(8,128)S(1)} copy-done((f32[2,128,256]{2,1,0:T(8,128)S(1)}, f32[2,128,256]{2,1,0:T(8,128)}, u32[]{:S(2)}) %copy-start.4) | copy-done | bytes 262168
  4.8 0.0 copy-start.5
  4.8 0.7 copy-done.5
  5.5 67.0 %shard_map.64 = f32[160,512]{1,0:T(8,128)S(1)} custom-call(s32[160,512]{1,0:T(8,128)S(1)} %copy-done, s32[160,512]{1,0:T(8,128)S(1)} %copy-done.1, s32[160,512]{1,0:T(8,128)S(1)} %copy-done.2, f32[2,128,256]{2,1,0:T(8,128)S(1)} %copy-done.4, f32[16,16,256]{2,1,0:T(8,128)S(1)} %copy-done.3, f32[16,256]{1,0:T(8,128)S(1)} %copy-done.5), custom_call_target="tpu_custom_call" | custom-call | tf_op jit(solution)/shard_map/pallas_call | solution.py:661
  72.5 0.7 copy.8
Async XLA Ops:
  0.0 1.0 %copy-start = (s32[160,512]{1,0:T(8,128)S(1)}, s32[160,512]{1,0:T(8,128)}, u32[]{:S(2)}) copy-start(s32[160,512]{1,0:T(8,128)} %refs_0_.1) | copy-start | bytes 983044
  1.0 1.0 %copy-start.1 = (s32[160,512]{1,0:T(8,128)S(1)}, s32[160,512]{1,0:T(8,128)}, u32[]{:S(2)}) copy-start(s32[160,512]{1,0:T(8,128)} %refs_1_.1) | copy-start | bytes 983044
  1.9 1.0 %copy-start.2 = (s32[160,512]{1,0:T(8,128)S(1)}, s32[160,512]{1,0:T(8,128)}, u32[]{:S(2)}) copy-start(s32[160,512]{1,0:T(8,128)} %refs_2_.1) | copy-start | bytes 983044
  2.9 0.9 %copy-start.3 = (f32[16,16,256]{2,1,0:T(8,128)S(1)}, f32[16,16,256]{2,1,0:T(8,128)}, u32[]{:S(2)}) copy-start(f32[16,16,256]{2,1,0:T(8,128)} %constant.7.clone.refs_4_) | copy-start | bytes 786436
  3.9 0.9 %copy-start.4 = (f32[2,128,256]{2,1,0:T(8,128)S(1)}, f32[2,128,256]{2,1,0:T(8,128)}, u32[]{:S(2)}) copy-start(f32[2,128,256]{2,1,0:T(8,128)} %constant.6.clone.refs_3_) | copy-start | bytes 786436
  4.8 0.7 copy-start.5

commit v2 on v1

--- a/solution.py
+++ b/solution.py
@@ -36,6 +36,7 @@
 FREQ = 256
 PAD = 48
 SHIFTS = (1, 2, 4, 8, 16, 32)
+UNROLL = 8
 HALVES = tuple(slice(h, h + 8) for h in range(0, SUB, 8))
 
 
@@ -87,16 +88,17 @@
 
 
 def steps(count, body):
-    if count <= 2:
+    if count <= UNROLL:
         for i in range(count):
             body(i)
     else:
 
         def step(i, carry):
-            body(i)
+            for j in range(UNROLL):
+                body(i * UNROLL + j)
             return carry
 
-        lax.fori_loop(0, count, step, 0)
+        lax.fori_loop(0, count // UNROLL, step, 0)
 
 
 def kernel(R, C, *refs):
@@ -665,7 +667,7 @@
             out_specs=pl.BlockSpec(memory_space=pl.ANY),
             scratch_shapes=scratch(R, C),
             compiler_params=pltpu.CompilerParams(
-                collective_id=0, has_side_effects=True, vmem_limit_bytes=48 * 1024 * 1024
+                collective_id=0, has_side_effects=True
             ),
         )(swath, coherence, counts, jnp.asarray(forward), jnp.asarray(backward), jnp.asarray(constants))
 

time: 73.5 us -> 57.5 us (0.78)
  Pallas kernels: 67 us -> 55.6 us
  local copies, waits for them, and re-layouts: 6.26 us -> 1.72 us
    pallas_call x1, Pallas kernels: 67 us -> 55.6 us  [body(): pl.pallas_call(functools.partial(kernel, R, C), out_shape=jax.ShapeDtypeS...]
    unnamed x13 -> x1, local copies, waits for them, and re-layouts: 6.26 us -> 1.72 us
where the time goes in v2:
time: 57.5 us; the launch traced here: 57.4 us
  Pallas kernels  55.6 us (97%)
  local copies, waits for them, and re-layouts  1.72 us (3%)
    pallas_call x1, Pallas kernels, body(): pl.pallas_call(functools.partial(kernel, R, C), out_shape=jax.ShapeDtypeS...  55.6 us
    unnamed x1, local copies, waits for them, and re-layouts  1.72 us

profile of v2, /device:TPU:1, one launch (start us, length us, event | category | flops | bytes accessed | tf_op | source)
XLA Modules:
  0.0 57.4 jit_solution(9452353930245622722)
XLA Ops:
  0.0 55.6 %shard_map.64 = f32[160,512]{1,0:T(8,128)} custom-call(s32[160,512]{1,0:T(8,128)} %refs_0_.1, s32[160,512]{1,0:T(8,128)} %refs_1_.1, s32[160,512]{1,0:T(8,128)} %refs_2_.1, f32[2,128,256]{2,1,0:T(8,128)} %constant.6.clone.refs_3_, f32[16,16,256]{2,1,0:T(8,128)} %constant.7.clone.refs_4_, f32[16,256]{1,0:T(8,128)} %constant.8.clone.refs_5_), custom_call_target="tpu_custom_call" | custom-call | tf_op jit(solution)/shard_map/pallas_call | solution.py:663
  55.6 1.7 %copy.8 = f32[160,512]{1,0:T(8,128)} copy(f32[160,512]{1,0:T(8,128)} %shard_map.64) | data formatting | bytes 655360

commit v3 on v2

--- a/solution.py
+++ b/solution.py
@@ -24,6 +24,7 @@
 
 STEP = 2**GRIDS
 HALO = 48
+NEAR = 16
 ROWS = 160
 COLS = 512
 CROWS = ROWS // STEP
@@ -119,6 +120,11 @@
         nat,
         left_pack,
         right_pack,
+        near_pack,
+        near_got,
+        in_left,
+        in_right,
+        outer,
         from_left,
         from_right,
         result,
@@ -178,31 +184,74 @@
     for copy in loads:
         copy.start()
 
-    for a in range(2):
-        for k in range(OWN_CHUNKS):
-            nat[a, k, ROWS:EXT, :] = jnp.zeros((EXT - ROWS, 128), F32)
-    from_left[...] = jnp.zeros((EXT, 128), F32)
-    from_right[...] = jnp.zeros((EXT, 128), F32)
-    near_left[...] = jnp.zeros(near_left.shape, F32)
-    near_right[...] = jnp.zeros(near_right.shape, F32)
-
     barrier = pltpu.get_barrier_semaphore()
-    for i in range(1, R):
-        pl.semaphore_signal(barrier, inc=1, device_id=(lax.rem(r + i, R), c), device_id_type=MESH)
-    for i in range(1, C):
+    for i in sorted(range(1, C), key=lambda i: -min(i, C - i)):
         pl.semaphore_signal(barrier, inc=1, device_id=(r, lax.rem(c + i, C)), device_id_type=MESH)
     for i in (1, R - 1):
         for j in (1, C - 1):
             pl.semaphore_signal(
                 barrier, inc=1, device_id=(lax.rem(r + i, R), lax.rem(c + j, C)), device_id_type=MESH
             )
+    for i in range(1, R):
+        pl.semaphore_signal(barrier, inc=1, device_id=(lax.rem(r + i, R), c), device_id_type=MESH)
+
+    is_up, is_down = r > 0, r < R - 1
+    is_left, is_right = c > 0, c < C - 1
+    chunks = slice(0, OWN_CHUNKS)
+    own, below, above = slice(0, ROWS), slice(ROWS, ROWS + HALO), slice(ROWS + HALO, EXT)
+    near_below, near_above = slice(ROWS, ROWS + NEAR), slice(EXT - NEAR, EXT)
+    far = slice(ROWS + NEAR, EXT - NEAR)
+    far_rows = EXT - ROWS - 2 * NEAR
+    far_below, far_above = slice(0, far_rows // 2), slice(far_rows // 2, far_rows)
+
+    def clear(ref, *where):
+        ref[where] = jnp.zeros(ref.at[where].shape, F32)
+
+    every = slice(None)
+    clear(nat, every, chunks, far)
+    clear(in_left, far)
+    clear(in_right, far)
+
+    @pl.when(jnp.logical_not(is_down))
+    def _():
+        clear(nat, every, chunks, near_below)
+        clear(outer, every, chunks, far_below)
+        for ref in (in_left, in_right):
+            clear(ref, near_below)
+        for ref in (from_left, from_right):
+            clear(ref, below)
+
+    @pl.when(jnp.logical_not(is_up))
+    def _():
+        clear(nat, every, chunks, near_above)
+        clear(outer, every, chunks, far_above)
+        for ref in (in_left, in_right):
+            clear(ref, near_above)
+        for ref in (from_left, from_right):
+            clear(ref, above)
+
+    @pl.when(jnp.logical_not(is_right))
+    def _():
+        clear(near_got, 0)
+        clear(in_right, near_below)
+        clear(in_right, near_above)
+        clear(from_right, slice(0, EXT))
+        clear(near_right, every)
+
+    @pl.when(jnp.logical_not(is_left))
+    def _():
+        clear(near_got, 1)
+        clear(in_left, near_below)
+        clear(in_left, near_above)
+        clear(from_left, slice(0, EXT))
+        clear(near_left, every)
 
     for copy in loads[:3]:
         copy.wait()
     lane = lax.broadcasted_iota(jnp.int32, (32, 128), 1)
 
     def prepare(i):
-        rows = pl.ds(pl.multiple_of(i * 32, 32), 32)
+        rows = slice(i * 32, i * 32 + 32)
         for k in range(OWN_CHUNKS):
             span = slice(128 * k, 128 * k + 128)
             level = coherence[rows, span].astype(F32) * (1.0 / (NCLASS - 1))
@@ -215,24 +264,42 @@
             if k == OWN_CHUNKS - 1:
                 right_pack[rows, :] = jnp.where(lane < 64, pltpu.roll(ph, 64, 1), q)
 
-    steps(ROWS // 32, prepare)
+    for i in range(ROWS // 32):
+        prepare(i)
+    quarter = ROWS // 4
+    lane = lax.broadcasted_iota(jnp.int32, (quarter, 128), 1)
+    packed = [jnp.zeros((quarter, 128), F32)] * 2
+    for g in range(4):
+        rows = slice(quarter * g, quarter * g + quarter)
+        turned = (pltpu.roll(left_pack[rows, :], NEAR * g, 1), pltpu.roll(right_pack[rows, :], NEAR * g + 80, 1))
+        packed = [jnp.where((lane & 48) == NEAR * g, x, y) for x, y in zip(turned, packed)]
+    near_pack[0] = packed[0]
+    near_pack[1] = packed[1]
     pl.semaphore_wait(barrier, R + C + 2)
 
+    both = jnp.logical_and
+    first_rows, last_rows = slice(0, NEAR), slice(ROWS - NEAR, ROWS)
     top, bottom = slice(0, HALO), slice(ROWS - HALO, ROWS)
-    own, below, above = slice(0, ROWS), slice(ROWS, ROWS + HALO), slice(ROWS + HALO, EXT)
-    chunks = slice(0, OWN_CHUNKS)
-    is_up, is_down = r > 0, r < R - 1
-    is_left, is_right = c > 0, c < C - 1
-    both = jnp.logical_and
+    top_far, bottom_far = slice(NEAR, HALO), slice(ROWS - HALO, ROWS - NEAR)
+    up_left, down_left = both(is_up, is_left), both(is_down, is_left)
+    up_right, down_right = both(is_up, is_right), both(is_down, is_right)
     plan = [
-        (is_up, -1, 0, nat.at[:, chunks, top, :], nat.at[:, chunks, below, :], is_down),
-        (is_down, 1, 0, nat.at[:, chunks, bottom, :], nat.at[:, chunks, above, :], is_up),
+        (is_left, 0, -1, near_pack.at[0], near_got.at[0], is_right),
+        (is_right, 0, 1, near_pack.at[1], near_got.at[1], is_left),
+        (up_left, -1, -1, left_pack.at[first_rows], in_right.at[near_below], down_right),
+        (down_left, 1, -1, left_pack.at[last_rows], in_right.at[near_above], up_right),
+        (up_right, -1, 1, right_pack.at[first_rows], in_left.at[near_below], down_left),
+        (down_right, 1, 1, right_pack.at[last_rows], in_left.at[near_above], up_left),
+        (is_up, -1, 0, nat.at[:, chunks, first_rows, :], nat.at[:, chunks, near_below, :], is_down),
+        (is_down, 1, 0, nat.at[:, chunks, last_rows, :], nat.at[:, chunks, near_above, :], is_up),
         (is_left, 0, -1, left_pack, from_right.at[own], is_right),
         (is_right, 0, 1, right_pack, from_left.at[own], is_left),
-        (both(is_up, is_left), -1, -1, left_pack.at[top], from_right.at[below], both(is_down, is_right)),
-        (both(is_down, is_left), 1, -1, left_pack.at[bottom], from_right.at[above], both(is_up, is_right)),
-        (both(is_up, is_right), -1, 1, right_pack.at[top], from_left.at[below], both(is_down, is_left)),
-        (both(is_down, is_right), 1, 1, right_pack.at[bottom], from_left.at[above], both(is_up, is_left)),
+        (up_left, -1, -1, left_pack.at[top], from_right.at[below], down_right),
+        (down_left, 1, -1, left_pack.at[bottom], from_right.at[above], up_right),
+        (up_right, -1, 1, right_pack.at[top], from_left.at[below], down_left),
+        (down_right, 1, 1, right_pack.at[bottom], from_left.at[above], up_left),
+        (is_up, -1, 0, nat.at[:, chunks, top_far, :], outer.at[:, chunks, far_below, :], is_down),
+        (is_down, 1, 0, nat.at[:, chunks, bottom_far, :], outer.at[:, chunks, far_above, :], is_up),
     ]
     halo_copies = []
     for i, (sends, dr, dc, source, target, receives) in enumerate(plan):
@@ -283,21 +350,27 @@
     spread[...] = jnp.where(at == jnp.where(to < CCOLS + 3, to + 8, to + 8 - WIDTH // STEP), 1.0, 0.0).astype(F32)
     ext[...] = jnp.zeros((PAD, FREQ), F32)
 
-    for _, receives, copy in halo_copies:
+    for _, receives, copy in halo_copies[:8]:
         pl.when(receives)(copy.wait_recv)
-
-    lane = lax.broadcasted_iota(jnp.int32, (SUB, 128), 1)
-    for p in range(STEP):
-        rows = pl.ds(p, SUB, stride=STEP)
-        for k in range(OWN_CHUNKS):
-            span = slice(128 * k, 128 * k + 128)
-            qual[p + 1, :, span] = nat.at[0, k][rows, :]
-            phase[p + 1, :, span] = nat.at[1, k][rows, :]
-        a, b = from_right[rows, :], from_left[rows, :]
-        qual[p + 1, :, COLS:WIDTH] = jnp.where(lane < 64, a, b)
-        phase[p + 1, :, COLS:WIDTH] = pltpu.roll(jnp.where(lane < 64, b, a), 64, 1)
-    wrap(qual, above=False)
-    wrap(phase, above=False)
+    lane = lax.broadcasted_iota(jnp.int32, (quarter, 128), 1)
+    for g in range(4):
+        rows = slice(quarter * g, quarter * g + quarter)
+        in_right[rows, :] = jnp.where((lane & 63) < NEAR, pltpu.roll(near_got[0], (128 - NEAR * g) % 128, 1), 0.0)
+        in_left[rows, :] = jnp.where((lane & 63) >= 64 - NEAR, pltpu.roll(near_got[1], 48 - NEAR * g, 1), 0.0)
+
+    def arrange(left, right):
+        lane = lax.broadcasted_iota(jnp.int32, (SUB, 128), 1)
+        for p in range(STEP):
+            rows = pl.ds(p, SUB, stride=STEP)
+            for k in range(OWN_CHUNKS):
+                span = slice(128 * k, 128 * k + 128)
+                qual[p + 1, :, span] = nat.at[0, k][rows, :]
+                phase[p + 1, :, span] = nat.at[1, k][rows, :]
+            a, b = right[rows, :], left[rows, :]
+            qual[p + 1, :, COLS:WIDTH] = jnp.where(lane < 64, a, b)
+            phase[p + 1, :, COLS:WIDTH] = pltpu.roll(jnp.where(lane < 64, b, a), 64, 1)
+        wrap(qual, above=False)
+        wrap(phase, above=False)
 
     def steep(u):
         return u - jnp.floor(u + 0.5)
@@ -309,10 +382,6 @@
             wr[p, h] = jnp.minimum(q, ahead(q, 1))
             sd[p + 1, h] = steep(phase[p + 2, h] - ph)
             sr[p, h] = steep(ahead(ph, 1) - ph)
-
-    steps(STEP, make_faces)
-    wrap(wd, below=False)
-    wrap(sd, below=False)
 
     def start_first(p):
         for h in HALVES:
@@ -323,8 +392,13 @@
             rdiv0[p, h] = rdiv
             v0[p + 1, h] = source * rdiv
 
-    steps(STEP, start_first)
-    wrap(v0)
+    def open_first(left, right):
+        arrange(left, right)
+        steps(STEP, make_faces)
+        wrap(wd, below=False)
+        wrap(sd, below=False)
+        steps(STEP, start_first)
+        wrap(v0)
 
     def restrict_fine():
         src, a1, b1 = levels[0][0], levels[0][1], levels[0][2]
@@ -438,7 +512,7 @@
 
         steps(STEP // 2, smooth)
 
-    def coarse_solve(turn):
+    def coarse_solve(turn, meanwhile):
         _, a3, b3, _, _, _ = levels[2]
         column = lax.broadcasted_iota(jnp.int32, (SUB, COLS), 1)
         line = lax.broadcasted_iota(jnp.int32, (SUB, COLS), 0)
@@ -510,6 +584,7 @@
         )
         pl.when(is_right)(rightward.start)
         pl.when(is_left)(leftward.start)
+        meanwhile()
         pl.when(is_left)(rightward.wait_recv)
         pl.when(is_right)(leftward.wait_recv)
         for copy in copies[R - 1 :]:
@@ -547,17 +622,27 @@
         coarse[...] = jnp.dot(values, spread[...], precision=HIGHEST, preferred_element_type=F32)
         return copies, rightward, leftward
 
-    def cycle(turn):
+    def descend():
         restrict_fine()
         for level in range(1, GRIDS):
             down(level)
-        sent = coarse_solve(turn)
+
+    def ascend():
         for level in range(GRIDS - 1, 0, -1):
             up(level)
         up_fine()
-        return sent
-
-    sent = [cycle(0)]
+
+    def widen():
+        for _, receives, copy in halo_copies[8:]:
+            pl.when(receives)(copy.wait_recv)
+        nat[:, chunks, far, :] = outer[...]
+        open_first(from_left, from_right)
+        descend()
+
+    open_first(in_left, in_right)
+    descend()
+    sent = [coarse_solve(0, widen)]
+    ascend()
     wrap(first)
 
     def reweight(p):
@@ -585,7 +670,9 @@
 
     steps(STEP, start_second)
     wrap(v0)
-    sent.append(cycle(1))
+    descend()
+    sent.append(coarse_solve(1, lambda: None))
+    ascend()
 
     outs = []
     for k in range(OWN_CHUNKS):
@@ -620,6 +707,11 @@
         pltpu.VMEM((2, OWN_CHUNKS, EXT, 128), F32),
         pltpu.VMEM((ROWS, 128), F32),
         pltpu.VMEM((ROWS, 128), F32),
+        pltpu.VMEM((2, ROWS // 4, 128), F32),
+        pltpu.VMEM((2, ROWS // 4, 128), F32),
+        pltpu.VMEM((EXT, 128), F32),
+        pltpu.VMEM((EXT, 128), F32),
+        pltpu.VMEM((2, OWN_CHUNKS, EXT - ROWS - 2 * NEAR, 128), F32),
         pltpu.VMEM((EXT, 128), F32),
         pltpu.VMEM((EXT, 128), F32),
         pltpu.VMEM((OWN_CHUNKS, EXT, 128), F32),
@@ -642,8 +734,8 @@
         pltpu.VMEM((4, CCOLS, FREQ), F32),
         pltpu.VMEM((2, C, 2, FREQ), F32),
         pltpu.SemaphoreType.DMA((6,)),
-        pltpu.SemaphoreType.DMA((8,)),
-        pltpu.SemaphoreType.DMA((8,)),
+        pltpu.SemaphoreType.DMA((16,)),
+        pltpu.SemaphoreType.DMA((16,)),
         pltpu.SemaphoreType.DMA((2, R - 1)),
         pltpu.SemaphoreType.DMA((2, R - 1)),
         pltpu.SemaphoreType.DMA((2, C - 1)),

time: 57.5 us -> 52.8 us (0.918)
  Pallas kernels: 55.6 us -> 51 us
    pallas_call x1, Pallas kernels: 55.6 us -> 51 us  [body(): pl.pallas_call(functools.partial(kernel, R, C), out_shape=jax.ShapeDtypeS...]
where the time goes in v3:
time: 52.8 us; the launch traced here: 52.7 us
  Pallas kernels  51 us (97%)
  local copies, waits for them, and re-layouts  1.72 us (3%)
    pallas_call x1, Pallas kernels, body(): pl.pallas_call(functools.partial(kernel, R, C), out_shape=jax.ShapeDtypeS...  51 us
    unnamed x1, local copies, waits for them, and re-layouts  1.72 us

profile of v3, /device:TPU:1, one launch (start us, length us, event | category | flops | bytes accessed | tf_op | source)
XLA Modules:
  0.0 52.7 jit_solution(390006436150462869)
XLA Ops:
  0.0 51.0 %shard_map.64 = f32[160,512]{1,0:T(8,128)} custom-call(s32[160,512]{1,0:T(8,128)} %refs_0_.1, s32[160,512]{1,0:T(8,128)} %refs_1_.1, s32[160,512]{1,0:T(8,128)} %refs_2_.1, f32[2,128,256]{2,1,0:T(8,128)} %constant.6.clone.refs_3_, f32[16,16,256]{2,1,0:T(8,128)} %constant.7.clone.refs_4_, f32[16,256]{1,0:T(8,128)} %constant.8.clone.refs_5_), custom_call_target="tpu_custom_call" | custom-call | tf_op jit(solution)/shard_map/pallas_call | solution.py:755
  51.0 1.7 %copy.8 = f32[160,512]{1,0:T(8,128)} copy(f32[160,512]{1,0:T(8,128)} %shard_map.64) | data formatting | bytes 655360

commit v4 on v3

--- a/solution.py
+++ b/solution.py
@@ -136,6 +136,7 @@
         sr,
         v0,
         rdiv0,
+        base0,
         first,
         gd,
         gr,
@@ -143,8 +144,8 @@
     ) = refs
     levels = []
     for _ in range(3):
-        levels.append(rest[:6])
-        rest = rest[6:]
+        levels.append(rest[:7])
+        rest = rest[7:]
     (
         coarse,
         select,
@@ -420,7 +421,7 @@
     def down(level):
         s = 2**level
         count = STEP // s
-        src, a, b, rdiv, v, _ = levels[level - 1]
+        src, a, b, rdiv, v, _, _ = levels[level - 1]
 
         def smooth(p):
             for h in HALVES:
@@ -455,26 +456,12 @@
         if a_n is not None:
             wrap(a_n, below=False)
 
-    def up(level):
+    def settle(level):
         s = 2**level
         count = STEP // s
-        src, a, b, rdiv, v, out = levels[level - 1]
-
-        def add(i):
-            for h in HALVES:
-                if level == GRIDS - 1:
-                    x = coarse[h]
-                else:
-                    x = levels[level][5][i, h]
-                    column = lax.broadcasted_iota(jnp.int32, x.shape, 1)
-                    x = jnp.where((column & s) == 0, x, behind(x, s))
-                v[2 * i + 1, h] = v[2 * i + 1, h] + x
-                v[2 * i + 2, h] = v[2 * i + 2, h] + x
-
-        steps(count // 2, add)
-        wrap(v)
-
-        def smooth(i):
+        src, a, b, rdiv, v, base, _ = levels[level - 1]
+
+        def body(i):
             for h in HALVES:
                 va, v1, v2, vb = v[2 * i, h], v[2 * i + 1, h], v[2 * i + 2, h], v[2 * i + 3, h]
                 g0 = a[2 * i, h] * (v1 - va)
@@ -482,24 +469,13 @@
                 g2 = a[2 * i + 2, h] * (vb - v2)
                 f1 = b[2 * i, h] * (ahead(v1, s) - v1)
                 f2 = b[2 * i + 1, h] * (ahead(v2, s) - v2)
-                out[2 * i, h] = v1 + (src[2 * i, h] + g1 - g0 + f1 - behind(f1, s)) * rdiv[2 * i, h]
-                out[2 * i + 1, h] = v2 + (src[2 * i + 1, h] + g2 - g1 + f2 - behind(f2, s)) * rdiv[2 * i + 1, h]
-
-        steps(count // 2, smooth)
-
-    def up_fine():
-        def add(i):
-            for h in HALVES:
-                x = levels[0][5][i, h]
-                column = lax.broadcasted_iota(jnp.int32, x.shape, 1)
-                x = jnp.where((column & 1) == 0, x, behind(x, 1))
-                v0[2 * i + 1, h] = v0[2 * i + 1, h] + x
-                v0[2 * i + 2, h] = v0[2 * i + 2, h] + x
-
-        steps(STEP // 2, add)
-        wrap(v0)
-
-        def smooth(i):
+                base[2 * i, h] = v1 + (src[2 * i, h] + g1 - g0 + f1 - behind(f1, s)) * rdiv[2 * i, h]
+                base[2 * i + 1, h] = v2 + (src[2 * i + 1, h] + g2 - g1 + f2 - behind(f2, s)) * rdiv[2 * i + 1, h]
+
+        steps(count // 2, body)
+
+    def settle_fine():
+        def body(i):
             for h in HALVES:
                 va, v1, v2, vb = v0[2 * i, h], v0[2 * i + 1, h], v0[2 * i + 2, h], v0[2 * i + 3, h]
                 g0 = wd[2 * i, h] * (v1 - va - sd[2 * i, h])
@@ -507,13 +483,62 @@
                 g2 = wd[2 * i + 2, h] * (vb - v2 - sd[2 * i + 2, h])
                 f1 = wr[2 * i, h] * (ahead(v1, 1) - v1 - sr[2 * i, h])
                 f2 = wr[2 * i + 1, h] * (ahead(v2, 1) - v2 - sr[2 * i + 1, h])
-                first[2 * i + 1, h] = v1 + (g1 - g0 + f1 - behind(f1, 1)) * rdiv0[2 * i, h]
-                first[2 * i + 2, h] = v2 + (g2 - g1 + f2 - behind(f2, 1)) * rdiv0[2 * i + 1, h]
-
-        steps(STEP // 2, smooth)
-
-    def coarse_solve(turn, meanwhile):
-        _, a3, b3, _, _, _ = levels[2]
+                base0[2 * i, h] = v1 + (g1 - g0 + f1 - behind(f1, 1)) * rdiv0[2 * i, h]
+                base0[2 * i + 1, h] = v2 + (g2 - g1 + f2 - behind(f2, 1)) * rdiv0[2 * i + 1, h]
+
+        steps(STEP // 2, body)
+
+    def settle_all():
+        settle_fine()
+        for level in range(1, GRIDS):
+            settle(level)
+
+    def climb(level, put):
+        s = 2**level
+        count = STEP // s
+        if level:
+            _, a, b, rdiv, _, base, _ = levels[level - 1]
+        else:
+            a, b, rdiv, base = wd, wr, rdiv0, base0
+        if level == GRIDS - 1:
+            above_it, below_it = pltpu.roll(coarse[...], 1, 0), pltpu.roll(coarse[...], SUB - 1, 0)
+
+        def correction(i, h):
+            if level == GRIDS - 1:
+                return (above_it[h], coarse[h], below_it[h])[i + 1]
+            x = levels[level][6][i + 1, h]
+            column = lax.broadcasted_iota(jnp.int32, x.shape, 1)
+            return jnp.where((column & s) == 0, x, behind(x, s))
+
+        for h in HALVES:
+            x = correction(0, h)
+            upper = x - correction(-1, h)
+            for i in range(count // 2):
+                after = correction(i + 1, h)
+                lower = after - x
+                side = ahead(x, s) - x
+                f1, f2 = b[2 * i, h] * side, b[2 * i + 1, h] * side
+                put(2 * i, h, base[2 * i, h] + x + (f1 - behind(f1, s) - a[2 * i, h] * upper) * rdiv[2 * i, h])
+                put(
+                    2 * i + 1,
+                    h,
+                    base[2 * i + 1, h] + x + (f2 - behind(f2, s) + a[2 * i + 2, h] * lower) * rdiv[2 * i + 1, h],
+                )
+                x, upper = after, lower
+
+    def ascend(put_fine):
+        for level in range(GRIDS - 1, 0, -1):
+            out = levels[level - 1][6]
+
+            def put(p, h, x, out=out):
+                out[p + 1, h] = x
+
+            climb(level, put)
+            wrap(out)
+        climb(0, put_fine)
+
+    def coarse_solve(turn, meanwhile, later):
+        a3, b3 = levels[2][1:3]
         column = lax.broadcasted_iota(jnp.int32, (SUB, COLS), 1)
         line = lax.broadcasted_iota(jnp.int32, (SUB, COLS), 0)
         here = slice(0, COLS)
@@ -526,7 +551,7 @@
         spot = lax.broadcasted_iota(jnp.int32, (8, 128), 1)
         blocks[turn, r] = jnp.where(spot < 32, mine[0:8], jnp.where(spot < 64, mine[8:16], local))
         copies = []
-        for i in range(1, R):
+        for i in sorted(range(1, R), key=lambda i: -min(i, R - i)):
             copy = pltpu.make_async_remote_copy(
                 src_ref=blocks.at[turn, r],
                 dst_ref=blocks.at[turn, r],
@@ -537,6 +562,7 @@
             )
             copy.start()
             copies.append(copy)
+        meanwhile()
         for copy in copies:
             copy.wait_recv()
         every = blocks[turn].reshape(R * 8, 128).T
@@ -555,7 +581,7 @@
         near_send[turn, 0, 1:4, :] = hat[CCOLS - 3 : CCOLS]
         near_send[turn, 1, 0:3, :] = hat[0:3]
         near_send[turn, 1, 3:4, :] = total(3)
-        for i in range(1, C):
+        for i in sorted(range(1, C), key=lambda i: -min(i, C - i)):
             copy = pltpu.make_async_remote_copy(
                 src_ref=amps.at[turn, c],
                 dst_ref=amps.at[turn, c],
@@ -584,7 +610,7 @@
         )
         pl.when(is_right)(rightward.start)
         pl.when(is_left)(leftward.start)
-        meanwhile()
+        later()
         pl.when(is_left)(rightward.wait_recv)
         pl.when(is_right)(leftward.wait_recv)
         for copy in copies[R - 1 :]:
@@ -627,22 +653,28 @@
         for level in range(1, GRIDS):
             down(level)
 
-    def ascend():
-        for level in range(GRIDS - 1, 0, -1):
-            up(level)
-        up_fine()
-
     def widen():
         for _, receives, copy in halo_copies[8:]:
             pl.when(receives)(copy.wait_recv)
         nat[:, chunks, far, :] = outer[...]
         open_first(from_left, from_right)
+
+    def finish_wide():
         descend()
+        settle_all()
+
+    def put_first(p, h, x):
+        first[p + 1, h] = x
+
+    def put_result(p, h, x):
+        rows = pl.ds(STEP * h.start + p, 8, stride=STEP)
+        for k in range(OWN_CHUNKS):
+            result.at[k][rows, :] = x[:, 128 * k : 128 * k + 128] * TURN
 
     open_first(in_left, in_right)
     descend()
-    sent = [coarse_solve(0, widen)]
-    ascend()
+    sent = [coarse_solve(0, widen, finish_wide)]
+    ascend(put_first)
     wrap(first)
 
     def reweight(p):
@@ -671,14 +703,12 @@
     steps(STEP, start_second)
     wrap(v0)
     descend()
-    sent.append(coarse_solve(1, lambda: None))
-    ascend()
+    sent.append(coarse_solve(1, settle_all, lambda: None))
+    ascend(put_result)
 
     outs = []
     for k in range(OWN_CHUNKS):
         span = slice(128 * k, 128 * k + 128)
-        for p in range(STEP):
-            result.at[k][pl.ds(p, SUB, stride=STEP), :] = first[p + 1, :, span] * TURN
         copy = pltpu.make_async_copy(result.at[k, own, :], out_h.at[:, span], out_sem.at[k])
         copy.start()
         outs.append(copy)
@@ -717,10 +747,10 @@
         pltpu.VMEM((OWN_CHUNKS, EXT, 128), F32),
     ]
     padded, plain = STEP + 2, STEP
-    shapes += [field(n) for n in (padded, padded, padded, plain, padded, plain, padded, plain, padded, padded, plain)]
+    shapes += [field(n) for n in (padded, padded, padded, plain, padded, plain, padded, plain, plain, padded, padded, plain)]
     for level in range(1, GRIDS):
         n = STEP >> level
-        shapes += [field(m) for m in (n, n + 2, n, n, n + 2, n)]
+        shapes += [field(m) for m in (n, n + 2, n, n, n + 2, n, n + 2)]
     shapes += [
         pltpu.VMEM((SUB, WIDTH), F32),
         pltpu.VMEM((COLS, 128), F32),

time: 52.8 us -> 53.7 us (1.017)
  Pallas kernels: 51 us -> 51.9 us
    pallas_call x1, Pallas kernels: 51 us -> 51.9 us  [body(): pl.pallas_call(functools.partial(kernel, R, C), out_shape=jax.ShapeDtypeS...]
where the time goes in v4:
time: 53.7 us; the launch traced here: 53.6 us
  Pallas kernels  51.9 us (97%)
  local copies, waits for them, and re-layouts  1.72 us (3%)
    pallas_call x1, Pallas kernels, body(): pl.pallas_call(functools.partial(kernel, R, C), out_shape=jax.ShapeDtypeS...  51.9 us
    unnamed x1, local copies, waits for them, and re-layouts  1.72 us

profile of v4, /device:TPU:1, one launch (start us, length us, event | category | flops | bytes accessed | tf_op | source)
XLA Modules:
  0.0 53.6 jit_solution(17842774144390129062)
XLA Ops:
  0.0 51.9 %shard_map.64 = f32[160,512]{1,0:T(8,128)} custom-call(s32[160,512]{1,0:T(8,128)} %refs_0_.1, s32[160,512]{1,0:T(8,128)} %refs_1_.1, s32[160,512]{1,0:T(8,128)} %refs_2_.1, f32[2,128,256]{2,1,0:T(8,128)} %constant.6.clone.refs_3_, f32[16,16,256]{2,1,0:T(8,128)} %constant.7.clone.refs_4_, f32[16,256]{1,0:T(8,128)} %constant.8.clone.refs_5_), custom_call_target="tpu_custom_call" | custom-call | tf_op jit(solution)/shard_map/pallas_call | solution.py:785
  51.9 1.7 %copy.8 = f32[160,512]{1,0:T(8,128)} copy(f32[160,512]{1,0:T(8,128)} %shard_map.64) | data formatting | bytes 655360

commit v5 on v4

--- a/solution.py
+++ b/solution.py
@@ -125,8 +125,9 @@
         in_left,
         in_right,
         outer,
-        from_left,
-        from_right,
+        far_pack,
+        far_got,
+        far_corner,
         result,
         qual,
         phase,
@@ -199,7 +200,7 @@
     is_up, is_down = r > 0, r < R - 1
     is_left, is_right = c > 0, c < C - 1
     chunks = slice(0, OWN_CHUNKS)
-    own, below, above = slice(0, ROWS), slice(ROWS, ROWS + HALO), slice(ROWS + HALO, EXT)
+    own = slice(0, ROWS)
     near_below, near_above = slice(ROWS, ROWS + NEAR), slice(EXT - NEAR, EXT)
     far = slice(ROWS + NEAR, EXT - NEAR)
     far_rows = EXT - ROWS - 2 * NEAR
@@ -219,8 +220,7 @@
         clear(outer, every, chunks, far_below)
         for ref in (in_left, in_right):
             clear(ref, near_below)
-        for ref in (from_left, from_right):
-            clear(ref, below)
+        clear(far_corner, every, far_below)
 
     @pl.when(jnp.logical_not(is_up))
     def _():
@@ -228,15 +228,15 @@
         clear(outer, every, chunks, far_above)
         for ref in (in_left, in_right):
             clear(ref, near_above)
-        for ref in (from_left, from_right):
-            clear(ref, above)
+        clear(far_corner, every, far_above)
 
     @pl.when(jnp.logical_not(is_right))
     def _():
         clear(near_got, 0)
         clear(in_right, near_below)
         clear(in_right, near_above)
-        clear(from_right, slice(0, EXT))
+        clear(far_got, 0)
+        clear(far_corner, 0)
         clear(near_right, every)
 
     @pl.when(jnp.logical_not(is_left))
@@ -244,7 +244,8 @@
         clear(near_got, 1)
         clear(in_left, near_below)
         clear(in_left, near_above)
-        clear(from_left, slice(0, EXT))
+        clear(far_got, 1)
+        clear(far_corner, 1)
         clear(near_left, every)
 
     for copy in loads[:3]:
@@ -276,11 +277,15 @@
         packed = [jnp.where((lane & 48) == NEAR * g, x, y) for x, y in zip(turned, packed)]
     near_pack[0] = packed[0]
     near_pack[1] = packed[1]
+    half = ROWS // 2
+    lane = lax.broadcasted_iota(jnp.int32, (half, 128), 1)
+    for i, pack in enumerate((left_pack, right_pack)):
+        x, y = pltpu.roll(pack[0:half, :], 128 - NEAR, 1), pltpu.roll(pack[half:ROWS, :], NEAR, 1)
+        far_pack[i] = jnp.where((lane & 32) == 0, x, y)
     pl.semaphore_wait(barrier, R + C + 2)
 
     both = jnp.logical_and
     first_rows, last_rows = slice(0, NEAR), slice(ROWS - NEAR, ROWS)
-    top, bottom = slice(0, HALO), slice(ROWS - HALO, ROWS)
     top_far, bottom_far = slice(NEAR, HALO), slice(ROWS - HALO, ROWS - NEAR)
     up_left, down_left = both(is_up, is_left), both(is_down, is_left)
     up_right, down_right = both(is_up, is_right), both(is_down, is_right)
@@ -293,12 +298,12 @@
         (down_right, 1, 1, right_pack.at[last_rows], in_left.at[near_above], up_left),
         (is_up, -1, 0, nat.at[:, chunks, first_rows, :], nat.at[:, chunks, near_below, :], is_down),
         (is_down, 1, 0, nat.at[:, chunks, last_rows, :], nat.at[:, chunks, near_above, :], is_up),
-        (is_left, 0, -1, left_pack, from_right.at[own], is_right),
-        (is_right, 0, 1, right_pack, from_left.at[own], is_left),
-        (up_left, -1, -1, left_pack.at[top], from_right.at[below], down_right),
-        (down_left, 1, -1, left_pack.at[bottom], from_right.at[above], up_right),
-        (up_right, -1, 1, right_pack.at[top], from_left.at[below], down_left),
-        (down_right, 1, 1, right_pack.at[bottom], from_left.at[above], up_left),
+        (is_left, 0, -1, far_pack.at[0], far_got.at[0], is_right),
+        (is_right, 0, 1, far_pack.at[1], far_got.at[1], is_left),
+        (up_left, -1, -1, left_pack.at[top_far], far_corner.at[0, far_below], down_right),
+        (down_left, 1, -1, left_pack.at[bottom_far], far_corner.at[0, far_above], up_right),
+        (up_right, -1, 1, right_pack.at[top_far], far_corner.at[1, far_below], down_left),
+        (down_right, 1, 1, right_pack.at[bottom_far], far_corner.at[1, far_above], up_left),
         (is_up, -1, 0, nat.at[:, chunks, top_far, :], outer.at[:, chunks, far_below, :], is_down),
         (is_down, 1, 0, nat.at[:, chunks, bottom_far, :], outer.at[:, chunks, far_above, :], is_up),
     ]
@@ -359,7 +364,7 @@
         in_right[rows, :] = jnp.where((lane & 63) < NEAR, pltpu.roll(near_got[0], (128 - NEAR * g) % 128, 1), 0.0)
         in_left[rows, :] = jnp.where((lane & 63) >= 64 - NEAR, pltpu.roll(near_got[1], 48 - NEAR * g, 1), 0.0)
 
-    def arrange(left, right):
+    def arrange():
         lane = lax.broadcasted_iota(jnp.int32, (SUB, 128), 1)
         for p in range(STEP):
             rows = pl.ds(p, SUB, stride=STEP)
@@ -367,7 +372,7 @@
                 span = slice(128 * k, 128 * k + 128)
                 qual[p + 1, :, span] = nat.at[0, k][rows, :]
                 phase[p + 1, :, span] = nat.at[1, k][rows, :]
-            a, b = right[rows, :], left[rows, :]
+            a, b = in_right[rows, :], in_left[rows, :]
             qual[p + 1, :, COLS:WIDTH] = jnp.where(lane < 64, a, b)
             phase[p + 1, :, COLS:WIDTH] = pltpu.roll(jnp.where(lane < 64, b, a), 64, 1)
         wrap(qual, above=False)
@@ -393,8 +398,8 @@
             rdiv0[p, h] = rdiv
             v0[p + 1, h] = source * rdiv
 
-    def open_first(left, right):
-        arrange(left, right)
+    def open_first():
+        arrange()
         steps(STEP, make_faces)
         wrap(wd, below=False)
         wrap(sd, below=False)
@@ -537,7 +542,7 @@
             wrap(out)
         climb(0, put_fine)
 
-    def coarse_solve(turn, meanwhile, later):
+    def coarse_solve(turn, meanwhile):
         a3, b3 = levels[2][1:3]
         column = lax.broadcasted_iota(jnp.int32, (SUB, COLS), 1)
         line = lax.broadcasted_iota(jnp.int32, (SUB, COLS), 0)
@@ -562,7 +567,6 @@
             )
             copy.start()
             copies.append(copy)
-        meanwhile()
         for copy in copies:
             copy.wait_recv()
         every = blocks[turn].reshape(R * 8, 128).T
@@ -610,7 +614,7 @@
         )
         pl.when(is_right)(rightward.start)
         pl.when(is_left)(leftward.start)
-        later()
+        meanwhile()
         pl.when(is_left)(rightward.wait_recv)
         pl.when(is_right)(leftward.wait_recv)
         for copy in copies[R - 1 :]:
@@ -657,9 +661,14 @@
         for _, receives, copy in halo_copies[8:]:
             pl.when(receives)(copy.wait_recv)
         nat[:, chunks, far, :] = outer[...]
-        open_first(from_left, from_right)
-
-    def finish_wide():
+        lane = lax.broadcasted_iota(jnp.int32, (half, 128), 1) & 63
+        for i, ref in enumerate((in_right, in_left)):
+            ref[far, :] = far_corner[i]
+            for g in range(2):
+                rows = slice(half * g, half * g + half)
+                x = pltpu.roll(far_got[i], NEAR if g == 0 else 128 - NEAR, 1)
+                ref[rows, :] = jnp.where((lane >= NEAR) & (lane < HALO), x, ref[rows, :])
+        open_first()
         descend()
         settle_all()
 
@@ -671,9 +680,9 @@
         for k in range(OWN_CHUNKS):
             result.at[k][rows, :] = x[:, 128 * k : 128 * k + 128] * TURN
 
-    open_first(in_left, in_right)
+    open_first()
     descend()
-    sent = [coarse_solve(0, widen, finish_wide)]
+    sent = [coarse_solve(0, widen)]
     ascend(put_first)
     wrap(first)
 
@@ -703,7 +712,7 @@
     steps(STEP, start_second)
     wrap(v0)
     descend()
-    sent.append(coarse_solve(1, settle_all, lambda: None))
+    sent.append(coarse_solve(1, settle_all))
     ascend(put_result)
 
     outs = []
@@ -742,8 +751,9 @@
         pltpu.VMEM((EXT, 128), F32),
         pltpu.VMEM((EXT, 128), F32),
         pltpu.VMEM((2, OWN_CHUNKS, EXT - ROWS - 2 * NEAR, 128), F32),
-        pltpu.VMEM((EXT, 128), F32),
-        pltpu.VMEM((EXT, 128), F32),
+        pltpu.VMEM((2, ROWS // 2, 128), F32),
+        pltpu.VMEM((2, ROWS // 2, 128), F32),
+        pltpu.VMEM((2, EXT - ROWS - 2 * NEAR, 128), F32),
         pltpu.VMEM((OWN_CHUNKS, EXT, 128), F32),
     ]
     padded, plain = STEP + 2, STEP

time: 53.7 us -> 52 us (0.968)
  Pallas kernels: 51.9 us -> 50.1 us
    pallas_call x1, Pallas kernels: 51.9 us -> 50.1 us  [body(): pl.pallas_call(functools.partial(kernel, R, C), out_shape=jax.ShapeDtypeS...]
where the time goes in v5:
time: 52 us; the launch traced here: 51.9 us
  Pallas kernels  50.1 us (96%)
  local copies, waits for them, and re-layouts  1.72 us (3%)
    pallas_call x1, Pallas kernels, body(): pl.pallas_call(functools.partial(kernel, R, C), out_shape=jax.ShapeDtypeS...  50.1 us
    unnamed x1, local copies, waits for them, and re-layouts  1.72 us

profile of v5, /device:TPU:1, one launch (start us, length us, event | category | flops | bytes accessed | tf_op | source)
XLA Modules:
  0.0 51.9 jit_solution(3165539302079320614)
XLA Ops:
  0.0 50.1 %shard_map.64 = f32[160,512]{1,0:T(8,128)} custom-call(s32[160,512]{1,0:T(8,128)} %refs_0_.1, s32[160,512]{1,0:T(8,128)} %refs_1_.1, s32[160,512]{1,0:T(8,128)} %refs_2_.1, f32[2,128,256]{2,1,0:T(8,128)} %constant.6.clone.refs_3_, f32[16,16,256]{2,1,0:T(8,128)} %constant.7.clone.refs_4_, f32[16,256]{1,0:T(8,128)} %constant.8.clone.refs_5_), custom_call_target="tpu_custom_call" | custom-call | tf_op jit(solution)/shard_map/pallas_call | solution.py:795
  50.1 1.7 %copy.8 = f32[160,512]{1,0:T(8,128)} copy(f32[160,512]{1,0:T(8,128)} %shard_map.64) | data formatting | bytes 655360

commit v6 on v5

--- a/solution.py
+++ b/solution.py
@@ -37,7 +37,7 @@
 FREQ = 256
 PAD = 48
 SHIFTS = (1, 2, 4, 8, 16, 32)
-UNROLL = 8
+UNROLL = 16
 HALVES = tuple(slice(h, h + 8) for h in range(0, SUB, 8))
 
 

time: 52 us -> 50.3 us (0.967)
  Pallas kernels: 50.1 us -> 48.4 us
    pallas_call x1, Pallas kernels: 50.1 us -> 48.4 us  [body(): pl.pallas_call(functools.partial(kernel, R, C), out_shape=jax.ShapeDtypeS...]
where the time goes in v6:
time: 50.3 us; the launch traced here: 50.1 us
  Pallas kernels  48.4 us (96%)
  local copies, waits for them, and re-layouts  1.72 us (3%)
    pallas_call x1, Pallas kernels, body(): pl.pallas_call(functools.partial(kernel, R, C), out_shape=jax.ShapeDtypeS...  48.4 us
    unnamed x1, local copies, waits for them, and re-layouts  1.72 us

profile of v6, /device:TPU:1, one launch (start us, length us, event | category | flops | bytes accessed | tf_op | source)
XLA Modules:
  0.0 50.1 jit_solution(14351756832630867493)
XLA Ops:
  0.0 48.4 %shard_map.64 = f32[160,512]{1,0:T(8,128)} custom-call(s32[160,512]{1,0:T(8,128)} %refs_0_.1, s32[160,512]{1,0:T(8,128)} %refs_1_.1, s32[160,512]{1,0:T(8,128)} %refs_2_.1, f32[2,128,256]{2,1,0:T(8,128)} %constant.6.clone.refs_3_, f32[16,16,256]{2,1,0:T(8,128)} %constant.7.clone.refs_4_, f32[16,256]{1,0:T(8,128)} %constant.8.clone.refs_5_), custom_call_target="tpu_custom_call" | custom-call | tf_op jit(solution)/shard_map/pallas_call | solution.py:795
  48.4 1.7 %copy.8 = f32[160,512]{1,0:T(8,128)} copy(f32[160,512]{1,0:T(8,128)} %shard_map.64) | data formatting | bytes 655360
